TPU v7x, 256 devices: a whole 4x4x8 slice. The times are simulated.
256 devices in a mesh: gx: 32 (over x_hi, z, core), gy: 8 (over x_lo, y).
Axes of the slice: x: 4 (x_hi: 2, x_lo: 2; x = x_hi * 2 + x_lo), y: 4, z: 8, core: 2. Of those that a mesh axis runs over, the one named last changes fastest.
Arguments:
- positions: float32 [3, 131072], P(None, ('gx', 'gy')), as said below
- species: int32 [131072], P(('gx', 'gy')), may hold values from 0 to 7
- send_lists: int32 [32, 8, 8, 32], P('gx', 'gy'), may hold values from 0 to 511, as said below
- cell_pairs: int32 [32, 8, 32, 2], P('gx', 'gy'), may hold values from 0 to 23, as said below
- block_count: int32 [32, 8], P('gx', 'gy'), may hold values from 24 to 32, as said below
- embed: float32 [8, 128], replicated, may hold values from -6 to 6
- radial_one: float32 [2, 8, 128], replicated, may hold values from -2 to 2
- mix_one: float32 [5, 128, 128], replicated, may hold values from -0.5 to 0.5
- radial_two: float32 [2, 8, 128], replicated, may hold values from -2 to 2
- mix_two: float32 [2, 128, 128], replicated, may hold values from -0.5 to 0.5
- readout: float32 [2, 128], replicated, may hold values from -0.5 to 0.5
Outputs:
- forces: float32 [3, 131072], P(None, ('gx', 'gy'))
- site_energy: float32 [131072], P(('gx', 'gy'))
Inputs may be any that keep to these rules, and one draw needn't show every extreme that they name: `positions`: every coordinate lies in 0 to 5120^(1/3) in its owner's frame. `send_lists`: each entry names 32 distinct atoms of the sending device, as indices 0 to 511 among its own atoms. `cell_pairs`: column 0 is an owned cell 0 to 15, column 1 a cell 0 to 23 of the extended table; the first 24 slots of a device name every extended cell once in column 1. `block_count`: the number of used leading slots of each device; some device uses all 32 and some only 24.
All inputs are finite; a program needn't handle non-finite values.
Results may differ from a plain program's by a relative error of at most 0.0003.
Values sent between devices are 32-bit elements; how exact they have to be, the bound alone decides.
No kernel may reach another device: no remote copies, remote signals or barrier semaphores. Data moves between devices by JAX's collectives and lax.ppermute only.
A program may use at most 64 MiB of HBM per device.

v0:
```python
import jax
import jax.numpy as jnp
import numpy as np
from jax import lax
from jax.sharding import PartitionSpec as P

NB = 8
CELL = 32


highest = lax.Precision.HIGHEST
cutoff_sq = 25.0
pair_scale = 0.5
steps_x = np.array([-1, -1, -1, 0, 0, 1, 1, 1])
steps_y = np.array([-1, 0, 1, -1, 1, -1, 0, 1])


def extended(cells, sides, width):
    for axis, dim in sides:
        count = lax.axis_size(axis)
        head = lax.slice_in_dim(cells, 0, width, axis=dim)
        tail = lax.slice_in_dim(cells, cells.shape[dim] - width, cells.shape[dim], axis=dim)
        cells = jnp.concatenate(
            [
                lax.ppermute(tail, axis, [(i, (i + 1) % count) for i in range(count)]),
                cells,
                lax.ppermute(head, axis, [((i + 1) % count, i) for i in range(count)]),
            ],
            axis=dim,
        )
    return cells


def matmul(left, right):
    return jnp.dot(left, right, precision=highest, preferred_element_type=jnp.float32)


def frame_side(atoms_dev):
    return float((atoms_dev * 10.0) ** (1.0 / 3.0))


def ghost_shift(ghost, side):
    along_x = jnp.repeat(jnp.asarray(steps_x * side, jnp.float32), ghost)
    along_y = jnp.repeat(jnp.asarray(steps_y * side, jnp.float32), ghost)
    return jnp.stack([along_x, along_y, jnp.zeros_like(along_x)])


def pair_basis(pos_recv, pos_send, same):
    separation = pos_send[:, None, :] - pos_recv[:, :, None]
    squared = jnp.sum(separation * separation, axis=0)
    spacing = cutoff_sq / (NB - 1)
    centers = jnp.arange(NB, dtype=jnp.float32) * spacing
    keepers = 1.0 - same * jnp.eye(pos_recv.shape[1], dtype=jnp.float32)
    envelope = jnp.square(jnp.maximum(1.0 - squared / cutoff_sq, 0.0)) * keepers
    radial = envelope[None] * jnp.exp(
        -jnp.square((squared[None] - centers[:, None, None]) / spacing)
    )
    return (radial, radial[:, None] * separation[None])


def block_one(pos_recv, pos_send, feat_send, same, radial_w):
    radial, oriented = pair_basis(pos_recv, pos_send, same)
    plain_part = jnp.einsum("bij,cj->bci", radial, feat_send, precision=highest)
    vector_part = jnp.einsum("baij,cj->baci", oriented, feat_send, precision=highest)
    scalar_out = jnp.einsum("bc,bci->ci", radial_w[0], plain_part, precision=highest)
    vector_out = jnp.einsum("bc,baci->aci", radial_w[1], vector_part, precision=highest)
    return (pair_scale * scalar_out, pair_scale * vector_out)


def block_two(pos_recv, pos_send, feat_send, same, radial_w):
    radial, oriented = pair_basis(pos_recv, pos_send, same)
    channels = radial_w.shape[2]
    scal_send = feat_send[:channels]
    vect_send = feat_send[channels:].reshape(3, channels, feat_send.shape[1])
    plain_part = jnp.einsum("bij,cj->bci", radial, scal_send, precision=highest)
    cross_part = jnp.einsum("baij,acj->bci", oriented, vect_send, precision=highest)
    total = jnp.einsum("bc,bci->ci", radial_w[0], plain_part, precision=highest)
    total = total + jnp.einsum("bc,bci->ci", radial_w[1], cross_part, precision=highest)
    return (pair_scale * total,)


def update_one(acc_scal, acc_vect, start, mix_one):
    power = jnp.sum(acc_vect * acc_vect, axis=0)
    scal_new = jax.nn.silu(matmul(mix_one[0], acc_scal) + matmul(mix_one[1], power)) + matmul(
        mix_one[2], start
    )
    gating = jax.nn.sigmoid(matmul(mix_one[4], acc_scal))
    vect_new = jnp.einsum("cd,adi->aci", mix_one[3], acc_vect, precision=highest) * gating[None]
    return (scal_new, vect_new)


def update_two(acc_scal, previous, mix_two):
    return jax.nn.silu(matmul(mix_two[0], acc_scal)) + matmul(mix_two[1], previous)


def cut_piece(whole, offset):
    return lax.dynamic_slice_in_dim(whole, offset, CELL, whole.ndim - 1)


def add_piece(whole, piece, offset):
    last_axis = whole.ndim - 1
    current = lax.dynamic_slice_in_dim(whole, offset, piece.shape[-1], last_axis)
    return lax.dynamic_update_slice_in_dim(whole, current + piece, offset, last_axis)


def loop_blocks(count, total_slots, stepper, initial):

    def padded_step(slot, running):
        return stepper(slot, running, (slot < count).astype(jnp.float32))

    return lax.fori_loop(0, total_slots, padded_step, initial)


def forward_layer(block_fn, own_pos, ext_pos, ext_feat, pairs, count, radial_w, initial):

    def stepper(slot, running, weight):
        receiver = pairs[slot, 0] * CELL
        sender = pairs[slot, 1] * CELL
        same = (pairs[slot, 0] == pairs[slot, 1]).astype(jnp.float32)
        parts = block_fn(
            cut_piece(own_pos, receiver),
            cut_piece(ext_pos, sender),
            cut_piece(ext_feat, sender),
            same,
            radial_w,
        )
        return tuple(
            (add_piece(whole, weight * piece, receiver) for whole, piece in zip(running, parts))
        )

    return loop_blocks(count, pairs.shape[0], stepper, initial)


def backward_one(own_pos, ext_pos, ext_feat, pairs, count, radial_w, grad_scal, grad_vect):

    def stepper(slot, running, weight):
        grad_own, grad_ext = running
        receiver = pairs[slot, 0] * CELL
        sender = pairs[slot, 1] * CELL
        same = (pairs[slot, 0] == pairs[slot, 1]).astype(jnp.float32)
        feat_send = cut_piece(ext_feat, sender)

        def local_block(pos_recv, pos_send):
            return block_one(pos_recv, pos_send, feat_send, same, radial_w)

        unused, pullback = jax.vjp(
            local_block, cut_piece(own_pos, receiver), cut_piece(ext_pos, sender)
        )
        back_recv, back_send = pullback(
            (weight * cut_piece(grad_scal, receiver), weight * cut_piece(grad_vect, receiver))
        )
        return (add_piece(grad_own, back_recv, receiver), add_piece(grad_ext, back_send, sender))

    initial = (jnp.zeros_like(own_pos), jnp.zeros_like(ext_pos))
    return loop_blocks(count, pairs.shape[0], stepper, initial)


def backward_two(own_pos, ext_pos, ext_feat, pairs, count, radial_w, grad_acc):

    def stepper(slot, running, weight):
        grad_own, grad_ext, grad_feat = running
        receiver = pairs[slot, 0] * CELL
        sender = pairs[slot, 1] * CELL
        same = (pairs[slot, 0] == pairs[slot, 1]).astype(jnp.float32)

        def local_block(pos_recv, pos_send, feat_send):
            return block_two(pos_recv, pos_send, feat_send, same, radial_w)

        unused, pullback = jax.vjp(
            local_block,
            cut_piece(own_pos, receiver),
            cut_piece(ext_pos, sender),
            cut_piece(ext_feat, sender),
        )
        back_recv, back_send, back_feat = pullback((weight * cut_piece(grad_acc, receiver),))
        return (
            add_piece(grad_own, back_recv, receiver),
            add_piece(grad_ext, back_send, sender),
            add_piece(grad_feat, back_feat, sender),
        )

    initial = (jnp.zeros_like(own_pos), jnp.zeros_like(ext_pos), jnp.zeros_like(ext_feat))
    return loop_blocks(count, pairs.shape[0], stepper, initial)


def direction_grid(pieces):
    blank_block = jnp.zeros_like(pieces[:1])
    joined = jnp.concatenate([pieces[:4], blank_block, pieces[4:]], axis=0)
    return joined.reshape((3, 3) + pieces.shape[1:])


def fetch_rows(table, lists):
    picked = jnp.moveaxis(jnp.take(table, lists, axis=1), 1, 0)
    layout_grid = direction_grid(picked)
    along_y = extended(layout_grid, (("gy", 1),), 1)
    along_x = extended(along_y[:, 0::2], (("gx", 0),), 1)
    arrived = [
        along_x[0, 0],
        along_x[0, 1],
        along_x[0, 2],
        along_y[1, 0],
        along_y[1, 4],
        along_x[4, 0],
        along_x[4, 1],
        along_x[4, 2],
    ]
    return jnp.concatenate(arrived, axis=1)


def return_rows(ghost_grads, lists, own_grads):
    row_count = ghost_grads.shape[0]
    ghost = lists.shape[1]
    pieces = jnp.moveaxis(ghost_grads.reshape(row_count, 8, ghost), 1, 0)
    layout_grid = direction_grid(pieces)
    along_x = extended(layout_grid, (("gx", 0),), 1)
    empty_block = jnp.zeros_like(layout_grid[0, 0])
    onward = jnp.stack(
        [
            jnp.stack([along_x[0, 0], empty_block, along_x[0, 2]]),
            jnp.stack([layout_grid[1, 0], empty_block, layout_grid[1, 2]]),
            jnp.stack([along_x[4, 0], empty_block, along_x[4, 2]]),
        ]
    )
    along_y = extended(onward, (("gy", 1),), 1)
    arrived = [
        along_y[0, 0],
        along_x[0, 1],
        along_y[0, 4],
        along_y[1, 0],
        along_y[1, 4],
        along_y[2, 0],
        along_x[4, 1],
        along_y[2, 4],
    ]
    return own_grads.at[:, lists].add(jnp.stack(arrived, axis=1))


def shards(
    positions,
    species,
    send_lists,
    cell_pairs,
    block_count,
    embed,
    radial_one,
    mix_one,
    radial_two,
    mix_two,
    readout,
):
    lists = send_lists[0, 0]
    pairs = cell_pairs[0, 0]
    count = block_count[0, 0]
    atoms_dev = positions.shape[1]
    channels = embed.shape[1]
    kinds = jnp.arange(embed.shape[0], dtype=jnp.int32)
    onehot = (species[None, :] == kinds[:, None]).astype(jnp.float32)
    start = matmul(embed.T, onehot)
    shifts = ghost_shift(lists.shape[1], frame_side(atoms_dev))
    table_one = jnp.concatenate([positions, start], axis=0)
    ghosts_one = fetch_rows(table_one, lists)
    ghost_start = ghosts_one[3:]
    ext_pos = jnp.concatenate([positions, ghosts_one[:3] + shifts], axis=1)
    ext_start = jnp.concatenate([start, ghost_start], axis=1)
    zero_scal = jnp.zeros((channels, atoms_dev), jnp.float32)
    zero_vect = jnp.zeros((3, channels, atoms_dev), jnp.float32)
    acc_scal, acc_vect = forward_layer(
        block_one, positions, ext_pos, ext_start, pairs, count, radial_one, (zero_scal, zero_vect)
    )

    def first_update(scal_in, vect_in):
        return update_one(scal_in, vect_in, start, mix_one)

    (scal_one, vect_one), pull_one = jax.vjp(first_update, acc_scal, acc_vect)
    table_two = jnp.concatenate([scal_one, vect_one.reshape(3 * channels, atoms_dev)], axis=0)
    ext_two = jnp.concatenate([table_two, fetch_rows(table_two, lists)], axis=1)
    (acc_two,) = forward_layer(
        block_two, positions, ext_pos, ext_two, pairs, count, radial_two, (zero_scal,)
    )

    def second_update(acc_in, previous):
        return update_two(acc_in, previous, mix_two)

    scal_two, pull_two = jax.vjp(second_update, acc_two, scal_one)
    site_energy = matmul(readout[0], scal_one) + matmul(readout[1], scal_two)
    grad_acc_two, grad_prev = pull_two(jnp.broadcast_to(readout[1][:, None], scal_two.shape))
    grad_own_two, grad_ext_pos_two, grad_ext_feat = backward_two(
        positions, ext_pos, ext_two, pairs, count, radial_two, grad_acc_two
    )
    ghost_back = jnp.concatenate(
        [grad_ext_feat[:, atoms_dev:], grad_ext_pos_two[:, atoms_dev:]], axis=0
    )
    own_back = jnp.concatenate(
        [grad_ext_feat[:, :atoms_dev], grad_ext_pos_two[:, :atoms_dev] + grad_own_two], axis=0
    )
    returned = return_rows(ghost_back, lists, own_back)
    grad_scal = returned[:channels] + grad_prev + readout[0][:, None]
    grad_vect = returned[channels : 4 * channels].reshape(3, channels, atoms_dev)
    grad_pos = returned[4 * channels :]
    grad_acc_scal, grad_acc_vect = pull_one((grad_scal, grad_vect))
    grad_own_one, grad_ext_pos_one = backward_one(
        positions, ext_pos, ext_start, pairs, count, radial_one, grad_acc_scal, grad_acc_vect
    )
    grad_pos = grad_pos + grad_own_one + grad_ext_pos_one[:, :atoms_dev]
    grad_pos = return_rows(grad_ext_pos_one[:, atoms_dev:], lists, grad_pos)
    return (-grad_pos, site_energy)


def solution(mesh):
    in_specs = (
        P(None, ("gx", "gy")),
        P(("gx", "gy")),
        P("gx", "gy", None, None),
        P("gx", "gy", None, None),
        P("gx", "gy"),
        P(),
        P(),
        P(),
        P(),
        P(),
        P(),
    )
    out_specs = (P(None, ("gx", "gy")), P(("gx", "gy")))
    return jax.shard_map(shards, mesh=mesh, in_specs=in_specs, out_specs=out_specs, check_vma=False)
```

profile of v0, /device:TPU:6, one launch (start us, length us, event | category | flops | bytes accessed | tf_op | source)
XLA Modules:
  0.0 1159.9 jit_solution(1494157389242437898)
XLA Ops:
  5.7 1.7 collective-permute-start
  7.3 2.6 collective-permute-start.1
  10.3 4.4 collective-permute-done
  14.9 5.3 collective-permute-start.3
  20.3 3.3 collective-permute-done.3
  23.6 5.5 collective-permute-done.2
  30.0 243.2 %while.64 = (s32[]{:T(128)}, f32[128,512]{1,0:T(8,128)S(1)}, f32[3,128,512]{2,1,0:T(8,128)S(1)}, s32[32,2]{0,1:T(2,128)S(1)}, f32[128,768]{0,1:T(8,128)S(1)}, /*...) while((s32[]{:T(128)}, f32[128,512]{1,0:T(8,128)S(1)}, ...), condition=%wide.region_2.3_spmd, body=%wide.region_0.0_spmd.sunk | while | flops 50733076 | bytes 863381 | solution.py:111
  278.0 2.2 pad_maximum_fusion.1
  281.5 1.8 collective-permute-start.4
  283.3 6.3 collective-permute-start.5
  290.7 2.2 collective-permute-done.4
  293.5 5.3 collective-permute-start.7
  298.8 3.1 collective-permute-done.6
  307.0 243.8 %while.65 = (s32[]{:T(128)}, f32[128,512]{1,0:T(8,128)S(1)}, s32[32,2]{0,1:T(2,128)S(1)}, f32[512,768]{0,1:T(8,128)}, f32[3,768]{1,0:T(4,128)S(1)}, /*index=5*/f...) while((s32[]{:T(128)}, f32[128,512]{1,0:T(8,128)S(1)}, ...), condition=%wide.region_6.7_spmd, body=%wide.region_4.6_spmd.sunk | while | flops 50589716 | bytes 408249 | solution.py:111
  553.2 290.6 %while.66 = (s32[]{:T(128)}, f32[3,512]{1,0:T(4,128)S(1)}, f32[3,768]{1,0:T(4,128)S(1)}, f32[512,768]{0,1:T(8,128)S(1)}, s32[32,2]{0,1:T(2,128)S(1)}, /*index=5*...) while((s32[]{:T(128)}, f32[3,512]{1,0:T(4,128)S(1)}, ...), condition=%wide.region_15.16_spmd, body=%wide.region_7.15_spmd.sunk | while | flops 101193848 | bytes 856045 | solution.py:111
  844.4 5.4 collective-permute-start.9
  849.8 3.8 collective-permute-done.8
  855.8 6.2 collective-permute-start.11
  862.0 3.3 collective-permute-done.10
  869.8 2.9 scatter_fusion
  873.7 1.4 copy.143
  875.4 1.4 fusion.109
  876.9 1.6 fusion.107
  878.5 1.4 convolution_bitcast_fusion.7
  880.0 1.4 fusion.91
  881.4 3.2 fusion.90
  884.6 252.5 %while.67 = (s32[]{:T(128)}, f32[3,512]{1,0:T(4,128)S(1)}, f32[3,768]{1,0:T(4,128)S(1)}, s32[32,2]{0,1:T(2,128)S(1)}, f32[3,768]{1,0:T(4,128)S(1)}, /*index=5*/f...) while((s32[]{:T(128)}, f32[3,512]{1,0:T(4,128)S(1)}, ...), condition=%wide.region_26.27_spmd, body=%wide.region_18.26_spmd.sunk | while | flops 50788468 | bytes 499641 | solution.py:111
  1137.3 4.8 collective-permute-start.13
  1142.2 6.5 collective-permute-done.12
  1148.9 2.1 collective-permute-start.15
  1152.6 4.3 collective-permute-done.14
  1157.1 2.0 scatter_fusion.1
  (2261 shorter events, 643.9 us)
Async XLA Ops:
  0.6 1.5 copy-start
  5.0 5.0 copy-start.19
  5.0 5.1 copy-start.18
  5.7 9.1 collective-permute-start
  7.3 7.4 collective-permute-start.1
  14.9 8.7 collective-permute-start.3
  20.3 8.8 collective-permute-start.2
  23.6 6.0 copy-start.10
  30.0 243.2 %copy-start.8 = (f32[5,128,128]{2,1,0:T(8,128)S(1)}, f32[5,128,128]{2,1,0:T(8,128)}, u32[]{:S(2)}) copy-start(f32[5,128,128]{2,1,0:T(8,128)} %param.28) | copy-start | bytes 983044
  273.2 1.4 copy-start.11
  274.1 2.7 copy-start.2
  281.3 8.2 copy-start.17
  281.5 11.4 collective-permute-start.4
  283.3 9.7 collective-permute-start.5
  290.7 2.5 copy-start.5
  293.0 14.0 %copy-start.6 = (f32[2,8,128]{2,1,0:T(8,128)S(1)}, f32[2,8,128]{2,1,0:T(8,128)}, u32[]{:S(2)}) copy-start(f32[2,8,128]{2,1,0:T(8,128)} %param.29) | copy-start | bytes 24580
  293.1 8.8 collective-permute-start.6
  293.5 11.6 collective-permute-start.7
  307.0 243.8 %copy-start.16 = (f32[2,128,128]{2,1,0:T(8,128)S(1)}, f32[2,128,128]{2,1,0:T(8,128)}, u32[]{:S(2)}) copy-start(f32[2,128,128]{2,1,0:T(8,128)} %param.30) | copy-start | bytes 393220
  844.4 9.3 collective-permute-start.8
  844.4 9.3 collective-permute-start.9
  853.6 1.0 copy-start.15
  853.7 0.9 copy-start.14
  854.6 10.7 collective-permute-start.10
  854.9 1.0 copy-start.13
  855.8 11.3 collective-permute-start.11
  873.7 1.6 copy-start.3
  876.9 4.5 copy-start.1
  1137.3 11.5 collective-permute-start.13
  1142.1 6.7 collective-permute-start.12
  1148.9 3.7 collective-permute-start.15
  1151.1 5.8 collective-permute-start.14
  (4 other events, 2.8 us)
where the time goes:
time: 1180 us; the launch traced here: 1160 us
  loops' own time  419 us (36%)
  matrix products  304 us (26%)
  local copies, waits for them, and re-layouts  238 us (20%)
  other arithmetic  117 us (10%)
  starting transfers between devices  41.6 us (4%)
  waiting for transfers between devices  37.8 us (3%)
    another operation x4, loops' own time, loop_blocks(): return lax.fori_loop(0, total_slots, padded_step, initial)  419 us
    dot_general x96, matrix products, block_two(): jnp.einsum('baij,acj->bci', oriented, vect_send, precision=highest)  113 us
    dynamic_update_slice x224, local copies, waits for them, and re-layouts, add_piece(): lax.dynamic_update_slice_in_dim(whole, current + piece, offset, last_axis)  109 us
    dynamic_slice x128, local copies, waits for them, and re-layouts, stepper(): sender = pairs[slot, 1] * CELL  81.4 us
    dot_general x96, matrix products, block_two(): plain_part = jnp.einsum('bij,cj->bci', radial, scal_send, precision=highest)  80 us
    dot_general x64, matrix products, block_one(): jnp.einsum('baij,cj->baci', oriented, feat_send, precision=highest)  53.6 us
    dot_general x64, matrix products, block_one(): plain_part = jnp.einsum('bij,cj->bci', radial, feat_send, precision=highest)  42.9 us
    ppermute x8, starting transfers between devices, extended(): lax.ppermute(head, axis, [((i + 1) % count, i) for i in range(count)])  37.9 us
  transfers between devices with their start and end apart: 16, of which 10 were waited for; matrix products, arithmetic and copies ran while one was open for 1% of the time, Pallas kernels for 0%

commit v1 on v0

v1 whole, which is shorter than its diff:
```python
import functools

import jax
import jax.numpy as jnp
import numpy as np
from jax import lax
from jax.experimental import pallas as pl
from jax.experimental.pallas import tpu as pltpu
from jax.sharding import PartitionSpec as P

NB = 8
CELL = 32
CH = 128
LANES = 128
OWN = 16
EXT = 24
CUT2 = 25.0
STEPS_X = np.array([-1, -1, -1, 0, 0, 1, 1, 1])
STEPS_Y = np.array([-1, 0, 1, -1, 1, -1, 0, 1])
F32 = jnp.float32
BF16 = jnp.bfloat16
VMEM = pltpu.VMEM
SMEM = pltpu.SMEM
PARAMS = pltpu.CompilerParams(vmem_limit_bytes=48 * 1024 * 1024)
CHUNK = 128

NN = (((1,), (0,)), ((), ()))
NT = (((1,), (1,)), ((), ()))
TN = (((0,), (0,)), ((), ()))


def split(x):
    hi = x.astype(BF16)
    return hi, (x - hi.astype(F32)).astype(BF16)


def mm(a, b, dims):
    return lax.dot_general(a, b, dims, preferred_element_type=F32)


def mm3(a, b, dims):
    (ah, al), (bh, bl) = a, b
    return mm(ah, bh, dims) + (mm(ah, bl, dims) + mm(al, bh, dims))


def iota(shape, dim):
    return lax.broadcasted_iota(jnp.int32, shape, dim)


def geometry(r, c, weight, prc, xt):
    own = prc[pl.ds(pl.multiple_of(r * CELL, CELL), CELL), :]
    vec = [xt[t + 1, pl.ds(c, 1), :] - own[:, t : t + 1] for t in range(3)]
    sq = vec[0] * vec[0] + vec[1] * vec[1] + vec[2] * vec[2]
    lane = iota((CELL, LANES), 1)
    row = iota((CELL, LANES), 0)
    self_pair = jnp.logical_and(lane % CELL == row, r == c)
    keep = jnp.where(self_pair, 0.0, weight)
    edge = jnp.maximum(1.0 - sq * (1.0 / CUT2), 0.0)
    slope = edge * keep
    group = lane // CELL
    vk = jnp.where(group == 0, 1.0, jnp.where(group == 1, vec[0], jnp.where(group == 2, vec[1], vec[2])))
    scaled = sq * ((NB - 1) / CUT2)
    return edge * slope, slope, scaled, vk


def basis(scaled, n):
    off = scaled - float(n)
    return jnp.exp(-(off * off))


def pair_tile(env, scaled, vk):
    m = env * vk
    return jnp.concatenate([m * basis(scaled, n) for n in range(NB)], axis=0)


def pair_force(deriv, env, slope, scaled, vk):
    total = None
    moment = None
    for n in range(NB):
        term = deriv[n * CELL : (n + 1) * CELL] * basis(scaled, n)
        total = term if n == 0 else total + term
        if n == 1:
            moment = term
        elif n > 1:
            moment = moment + float(n) * term
    spacing = CUT2 / (NB - 1)
    direct = env * total
    by_sq = (-2.0 / CUT2) * slope * total - (2.0 / spacing) * env * (scaled * total - moment)
    by_sq = by_sq * vk
    by_sq = by_sq + pltpu.roll(by_sq, 64, 1)
    by_sq = by_sq + pltpu.roll(by_sq, 32, 1)
    return direct + 2.0 * vk * by_sq


def add_force(force, r, c, recv, send):
    rows = pl.ds(pl.multiple_of(r * CELL, CELL), CELL)
    recv[rows, :] += force
    send[pl.ds(c, 1), :] += jnp.sum(force, axis=0, keepdims=True)


def species_tile(c, xt):
    row = iota((4 * NB, LANES), 0)
    lane = iota((4 * NB, LANES), 1)
    kind = xt[0, pl.ds(c, 1), :].astype(jnp.int32)
    hit = jnp.logical_and(kind == row % NB, lane // CELL == row // NB)
    return jnp.where(hit, 1.0, 0.0).astype(BF16)


def species_weights(embed, radial):
    zero = jnp.zeros((NB, CH), F32)
    rows = []
    for n in range(NB):
        for k in range(4):
            part = embed * radial[min(k, 1), n : n + 1, :]
            rows.append(jnp.concatenate([part if j == k else zero for j in range(4)], axis=1))
    return split(jnp.concatenate(rows, axis=0))


def for_blocks(pairs, count, unroll, body):
    def step(i, carry):
        for k in range(unroll):
            slot = i * unroll + k
            weight = jnp.where(slot < count[0], 1.0, 0.0).astype(F32)
            body(pairs[2 * slot], pairs[2 * slot + 1], weight)
        return carry

    lax.fori_loop(0, (count[0] + unroll - 1) // unroll, step, 0)


def pack_kernel(pos, species, lists, out):
    kinds = species[...].astype(F32)
    table = jnp.concatenate([kinds, pos[...], jnp.zeros((4, kinds.shape[1]), F32)], axis=0)
    hi = table.astype(BF16)
    rest = table - hi.astype(F32)
    mid = rest.astype(BF16)
    low = (rest - mid.astype(F32)).astype(BF16)
    atoms = kinds.shape[1]
    hot = jnp.where(iota((atoms, lists.shape[1]), 0) == lists[...], 1.0, 0.0).astype(BF16)
    out[...] = mm(hi, hot, NN) + mm(mid, hot, NN) + mm(low, hot, NN)


def first_kernel(
    pairs, count, lists, xt, prc, embed, radial, mix, feat, sent, acc, gates, lifted, hist
):
    hist[...] = jnp.zeros_like(hist)

    def block(r, c, weight):
        env, slope, scaled, vk = geometry(r, c, weight, prc, xt)
        hi, lo = split(pair_tile(env, scaled, vk))
        hot = species_tile(c, xt)
        part = mm(hi, hot, NT) + mm(lo, hot, NT)
        rows = pl.ds(pl.multiple_of(r * CELL, CELL), CELL)
        for n in range(NB):
            hist[n, rows, :] += part[n * CELL : (n + 1) * CELL]

    for_blocks(pairs, count, 2, block)

    weights = species_weights(embed[...], radial)
    mix04 = split(jnp.concatenate([mix[0], mix[4]], axis=0))
    mix1 = split(mix[1])
    mix3 = split(mix[3])
    begin = split(mm3(split(embed[...]), split(mix[2]), NT))

    def chunk(i, carry):
        rows = pl.ds(pl.multiple_of(i * CHUNK, CHUNK), CHUNK)
        joined = jnp.concatenate([hist[n, rows, :] for n in range(NB)], axis=1)
        a = mm3(split(joined), weights, NN)
        acc[rows, :] = a
        a0 = a[:, :CH]
        a1 = [a[:, (t + 1) * CH : (t + 2) * CH] for t in range(3)]
        power = a1[0] * a1[0] + a1[1] * a1[1] + a1[2] * a1[2]
        both = mm3(split(a0), mix04, NT)
        z0 = both[:, :CH] + mm3(split(power), mix1, NT)
        gate = jax.nn.sigmoid(both[:, CH:])
        kind = prc[rows, :][:, 3:4].astype(jnp.int32)
        hot = jnp.where(kind == iota((CHUNK, NB), 1), 1.0, 0.0).astype(BF16)
        own = mm(hot, begin[0], NN) + mm(hot, begin[1], NN)
        lift = mm3(split(jnp.concatenate(a1, axis=0)), mix3, NT)
        lift = jnp.concatenate([lift[t * CHUNK : (t + 1) * CHUNK] for t in range(3)], axis=1)
        gates[rows, :] = jnp.concatenate([z0, gate], axis=1)
        lifted[rows, :] = lift
        feat[rows, :] = jnp.concatenate(
            [z0 * jax.nn.sigmoid(z0) + own, lift * jnp.concatenate([gate] * 3, axis=1)], axis=1
        )
        return carry

    lax.fori_loop(0, feat.shape[0] // CHUNK, chunk, 0)

    def gather(i, carry):
        for k in range(8):
            at = i * 8 + k
            sent[pl.ds(at, 1), :] = feat[pl.ds(lists[at], 1), :]
        return carry

    lax.fori_loop(0, sent.shape[0] // 8, gather, 0)


def cell_features(table, c):
    f = table[pl.ds(pl.multiple_of(c * CELL, CELL), CELL), :]
    hi, lo = split(f)
    zero = jnp.zeros((CELL, CH), BF16)

    def lay(x):
        rows = [jnp.concatenate([x[:, :CH], zero], axis=1)]
        rows += [jnp.concatenate([zero, x[:, (t + 1) * CH : (t + 2) * CH]], axis=1) for t in range(3)]
        return jnp.concatenate(rows, axis=0)

    return lay(hi), lay(lo)


def ghost_pieces(left, right, up, down):
    return (
        [right[k * CELL : (k + 1) * CELL] for k in range(3)]
        + [up[CELL : 2 * CELL], down[CELL : 2 * CELL]]
        + [left[k * CELL : (k + 1) * CELL] for k in range(3)]
    )


def second_kernel(
    pairs, count, xt, prc, feat, left, right, up, down, radial, mix, readout,
    energy, grad_own, grad_ghost, recv, send,
    table, acc, grad_acc, grad_table,
):
    atoms = feat.shape[0]
    table[0:atoms, :] = feat[...]
    for p, piece in enumerate(ghost_pieces(left, right, up, down)):
        table[atoms + p * CELL : atoms + (p + 1) * CELL, :] = piece
    acc[...] = jnp.zeros_like(acc)
    grad_table[...] = jnp.zeros_like(grad_table)
    recv[...] = jnp.zeros_like(recv)
    send[...] = jnp.zeros_like(send)

    def forward(r, c, weight):
        env, slope, scaled, vk = geometry(r, c, weight, prc, xt)
        prod = mm3(split(pair_tile(env, scaled, vk)), cell_features(table, c), NN)
        part = None
        for n in range(NB):
            rows = prod[n * CELL : (n + 1) * CELL]
            term = rows[:, :CH] * radial[0, n : n + 1, :] + rows[:, CH:] * radial[1, n : n + 1, :]
            part = term if n == 0 else part + term
        acc[pl.ds(pl.multiple_of(r * CELL, CELL), CELL), :] += part

    for_blocks(pairs, count, 2, forward)

    mix0 = split(mix[0])
    carry_w = readout[0:1, :] + mm3(split(readout[...]), split(mix[1]), NN)[1:2, :]
    row8 = iota((8, CH), 0)
    first = split(jnp.where(row8 == 0, carry_w, 0.0))
    second = split(jnp.where(row8 == 0, readout[1:2, :], 0.0))

    for i in range(atoms // CHUNK):
        rows = pl.ds(i * CHUNK, CHUNK)
        z = mm3(split(acc[rows, :]), mix0, NT)
        sg = jax.nn.sigmoid(z)
        s1 = feat[rows, :][:, :CH]
        energy[:, i * CHUNK : (i + 1) * CHUNK] = mm3(first, split(s1), NT) + mm3(second, split(z * sg), NT)
        gz = readout[1:2, :] * (sg * (1.0 + z * (1.0 - sg)))
        grad_acc[rows, :] = mm3(split(gz), mix0, NN)

    def backward(r, c, weight):
        env, slope, scaled, vk = geometry(r, c, weight, prc, xt)
        tile = split(pair_tile(env, scaled, vk))
        g = grad_acc[pl.ds(pl.multiple_of(r * CELL, CELL), CELL), :]
        u = split(
            jnp.concatenate(
                [
                    jnp.concatenate([g * radial[0, n : n + 1, :], g * radial[1, n : n + 1, :]], axis=1)
                    for n in range(NB)
                ],
                axis=0,
            )
        )
        gf = mm3(tile, u, TN)
        rows = pl.ds(pl.multiple_of(c * CELL, CELL), CELL)
        grad_table[rows, :] += jnp.concatenate(
            [gf[0:CELL, :CH]] + [gf[(t + 1) * CELL : (t + 2) * CELL, CH:] for t in range(3)], axis=1
        )
        deriv = mm3(u, cell_features(table, c), NT)
        add_force(pair_force(deriv, env, slope, scaled, vk), r, c, recv, send)

    for_blocks(pairs, count, 1, backward)
    grad_own[...] = grad_table[0:atoms, :]
    grad_ghost[...] = grad_table[atoms:, :]


def third_kernel(
    pairs, count, lists, xt, prc, grad_own, left, right, up, down, acc, gates, lifted,
    embed, radial, mix, mix_two, readout, recv_two, send_two,
    total, send,
    recv, quad, back_hi, back_lo,
):
    atoms = grad_own.shape[0]
    for p, piece in enumerate(ghost_pieces(left, right, up, down)):
        hi, lo = split(piece)
        back_hi[p * CELL : (p + 1) * CELL, :] = hi
        back_lo[p * CELL : (p + 1) * CELL, :] = lo
    recv[...] = recv_two[...]
    send[...] = send_two[...]
    weights = species_weights(embed[...], radial)
    mix04 = split(jnp.concatenate([mix[0], mix[4]], axis=0))
    mix1 = split(mix[1])
    mix3 = split(mix[3])
    carry_w = readout[0:1, :] + mm3(split(readout[...]), split(mix_two[1]), NN)[1:2, :]

    def chunk(i, carry):
        rows = pl.ds(pl.multiple_of(i * CHUNK, CHUNK), CHUNK)
        hot = jnp.where(iota((CHUNK, lists.shape[1]), 0) + i * CHUNK == lists[...], 1.0, 0.0).astype(BF16)
        g = grad_own[rows, :] + (mm(hot, back_hi[...], NN) + mm(hot, back_lo[...], NN))
        z0 = gates[rows, :][:, :CH]
        gate = gates[rows, :][:, CH:]
        gs = g[:, :CH] + carry_w
        sg = jax.nn.sigmoid(z0)
        dz0 = gs * (sg * (1.0 + z0 * (1.0 - sg)))
        gv = [g[:, (t + 1) * CH : (t + 2) * CH] for t in range(3)]
        y = [lifted[rows, :][:, t * CH : (t + 1) * CH] for t in range(3)]
        dgate = gv[0] * y[0] + gv[1] * y[1] + gv[2] * y[2]
        dz4 = dgate * gate * (1.0 - gate)
        da0 = mm3(split(jnp.concatenate([dz0, dz4], axis=1)), mix04, NN)
        dpower = 2.0 * mm3(split(dz0), mix1, NN)
        dy = mm3(split(jnp.concatenate([v * gate for v in gv], axis=0)), mix3, NN)
        a = acc[rows, :]
        parts = [da0] + [
            dy[t * CHUNK : (t + 1) * CHUNK] + a[:, (t + 1) * CH : (t + 2) * CH] * dpower for t in range(3)
        ]
        q = mm3(split(jnp.concatenate(parts, axis=1)), weights, NT)
        for n in range(NB):
            quad[n, rows, :] = q[:, n * 4 * NB : (n + 1) * 4 * NB]
        return carry

    lax.fori_loop(0, atoms // CHUNK, chunk, 0)

    def block(r, c, weight):
        env, slope, scaled, vk = geometry(r, c, weight, prc, xt)
        rows = pl.ds(pl.multiple_of(r * CELL, CELL), CELL)
        hi, lo = split(jnp.concatenate([quad[n, rows, :] for n in range(NB)], axis=0))
        hot = species_tile(c, xt)
        deriv = mm(hi, hot, NN) + mm(lo, hot, NN)
        add_force(pair_force(deriv, env, slope, scaled, vk), r, c, recv, send)

    for_blocks(pairs, count, 2, block)

    pick = jnp.where(iota((8, LANES), 0) + 1 == iota((8, LANES), 1) // CELL, 1.0, 0.0).astype(BF16)
    hi, lo = split(recv[...])
    total[...] = mm(pick, hi, NT) + mm(pick, lo, NT)


def last_kernel(total, own_send, back, lists, out):
    hi, lo = split(back[...])
    hot = jnp.where(iota((total.shape[1], lists.shape[1]), 0) == lists[...], 1.0, 0.0).astype(BF16)
    ghost = mm(hi, hot, NT) + mm(lo, hot, NT)
    out[...] = total[0:3, :] - own_send[...] - ghost[0:3, :]


def ring(axis, step):
    count = lax.axis_size(axis)
    return [(i, (i + step) % count) for i in range(count)]


def exchange(x):
    up = lax.ppermute(jnp.concatenate([x[2:3], x[4:5], x[7:8]]), "gy", ring("gy", 1))
    down = lax.ppermute(jnp.concatenate([x[0:1], x[3:4], x[5:6]]), "gy", ring("gy", -1))
    left = lax.ppermute(jnp.concatenate([up[0:1], x[1:2], down[0:1]]), "gx", ring("gx", -1))
    right = lax.ppermute(jnp.concatenate([up[2:3], x[6:7], down[2:3]]), "gx", ring("gx", 1))
    return left, right, up, down


def in_order(left, right, up, down):
    return jnp.concatenate([right, up[1:2], down[1:2], left])


def call(kernel, outs, specs, scratch=()):
    return pl.pallas_call(
        kernel,
        out_shape=[jax.ShapeDtypeStruct(s, F32) for s in outs],
        in_specs=[pl.BlockSpec(memory_space=s) for s in specs],
        out_specs=[pl.BlockSpec(memory_space=VMEM) for _ in outs],
        scratch_shapes=list(scratch),
        compiler_params=PARAMS,
    )


def shards(
    positions, species, send_lists, cell_pairs, block_count,
    embed, radial_one, mix_one, radial_two, mix_two, readout,
):
    atoms = positions.shape[1]
    side = float((atoms * 10.0) ** (1.0 / 3.0))
    pairs = cell_pairs.reshape(-1)
    count = block_count.reshape(-1)
    lists = send_lists.reshape(-1)
    lists_row = lists[None, :]
    half_one = 0.5 * radial_one
    half_two = 0.5 * radial_two
    ghosts = lists.shape[0]

    (packed,) = call(pack_kernel, [(8, ghosts)], [VMEM] * 3)(positions, species[None, :], lists_row)
    pieces = packed[:4].reshape(4, 8, CELL).transpose(1, 0, 2)
    arrived = in_order(*exchange(pieces))
    shift = np.zeros((8, 4, 1), np.float32)
    shift[:, 1, 0] = STEPS_X * side
    shift[:, 2, 0] = STEPS_Y * side
    arrived = arrived + jnp.asarray(shift)
    kinds = species.astype(F32)
    own_cells = jnp.concatenate([kinds[None], positions]).reshape(4, OWN, CELL)
    xt = jnp.tile(jnp.concatenate([own_cells, arrived.transpose(1, 0, 2)], axis=1), (1, 1, 4))
    prc = jnp.concatenate([positions, kinds[None], jnp.zeros((4, atoms), F32)]).T

    feat, sent, acc, gates, lifted = call(
        first_kernel,
        [(atoms, 4 * CH), (ghosts, 4 * CH), (atoms, 4 * CH), (atoms, 2 * CH), (atoms, 3 * CH)],
        [SMEM] * 3 + [VMEM] * 5,
        [pltpu.VMEM((NB, atoms, 4 * NB), F32)],
    )(pairs, count, lists, xt, prc, embed, half_one, mix_one)

    flat = lambda parts: [x.reshape(3 * CELL, 4 * CH) for x in parts]
    ghost_feat = flat(exchange(sent.reshape(8, CELL, 4 * CH)))
    energy, grad_own, grad_ghost, recv_two, send_two = call(
        second_kernel,
        [(8, atoms), (atoms, 4 * CH), (ghosts, 4 * CH), (atoms, LANES), (EXT, LANES)],
        [SMEM] * 2 + [VMEM] * 10,
        [
            pltpu.VMEM((atoms + ghosts, 4 * CH), F32),
            pltpu.VMEM((atoms, CH), F32),
            pltpu.VMEM((atoms, CH), F32),
            pltpu.VMEM((atoms + ghosts, 4 * CH), F32),
        ],
    )(pairs, count, xt, prc, feat, *ghost_feat, half_two, mix_two, readout)

    returned = flat(exchange(grad_ghost.reshape(8, CELL, 4 * CH)))
    total, send = call(
        third_kernel,
        [(8, atoms), (EXT, LANES)],
        [SMEM] * 2 + [VMEM] * 18,
        [
            pltpu.VMEM((atoms, LANES), F32),
            pltpu.VMEM((NB, atoms, 4 * NB), F32),
            pltpu.VMEM((ghosts, 4 * CH), BF16),
            pltpu.VMEM((ghosts, 4 * CH), BF16),
        ],
    )(
        pairs, count, lists_row, xt, prc, grad_own, *returned, acc, gates, lifted,
        embed, half_one, mix_one, mix_two, readout, recv_two, send_two,
    )

    back = in_order(*exchange(send[OWN:].reshape(8, 1, LANES)))
    back = back.reshape(8, 4, CELL).transpose(1, 0, 2)[1:].reshape(3, ghosts)
    own_send = send[:OWN].reshape(OWN, 4, CELL).transpose(1, 0, 2)[1:].reshape(3, atoms)
    (forces,) = call(last_kernel, [(3, atoms)], [VMEM] * 4)(
        total, own_send, jnp.concatenate([back, jnp.zeros((5, ghosts), F32)]), lists_row
    )
    return forces, energy[0]


def solution(mesh):
    both = P(("gx", "gy"))
    in_specs = (
        P(None, ("gx", "gy")),
        both,
        P("gx", "gy", None, None),
        P("gx", "gy", None, None),
        P("gx", "gy"),
    ) + (P(),) * 6
    out_specs = (P(None, ("gx", "gy")), both)
    return jax.shard_map(shards, mesh=mesh, in_specs=in_specs, out_specs=out_specs, check_vma=False)
```

time: 1180 us -> 122 us (0.10); the launches traced: 1160 us -> 120 us
  loops' own time: 419 us -> 0 us
  matrix products: 304 us -> 0 us
  local copies, waits for them, and re-layouts: 238 us -> 5.4 us
  other arithmetic: 117 us -> 0.4 us
  Pallas kernels: 0 us -> 52.1 us
  starting transfers between devices: 41.6 us -> 24.2 us
    another operation x4 -> x0, loops' own time: 419 us -> none  [loop_blocks(): return lax.fori_loop(0, total_slots, padded_step, initial)]
    dot_general x336 -> x0, matrix products: 304 us -> none  [the longest x96 113 us: block_two(): jnp.einsum('baij,acj->bci', oriented, vect_send, precision=highest)]
    dynamic_update_slice x224 -> x0, local copies, waits for them, and re-layouts: 109 us -> none  [add_piece(): lax.dynamic_update_slice_in_dim(whole, current + piece, offset, last_axis)]
    dynamic_slice x288 -> x0, local copies, waits for them, and re-layouts: 93.9 us -> none  [the longest x128 81.4 us: stepper(): sender = pairs[slot, 1] * CELL]
    pallas_call x0 -> x5, Pallas kernels: none -> 52.1 us  [the longest x1 29.7 us: shards(): call(second_kernel, [(8, atoms), (atoms, 4 * CH), (ghosts, 4 * CH), (atom...]
    mul x448 -> x2, other arithmetic: 38.8 us -> 0.01 us  [the longest x1 0.01 us: shards(): half_one = 0.5 * radial_one]
    transpose x32 -> x1, other arithmetic: 26.1 us -> 0.07 us  [shards(): arrived.transpose(1, 0, 2)]
    add x196 -> x0, other arithmetic: 18.2 us -> none  [the longest x192 17.5 us: add_piece(): current + piece]
where the time goes in v1:
time: 122 us; the launch traced here: 120 us
  Pallas kernels  52.1 us (43%)
  waiting for transfers between devices  36.6 us (30%)
  starting transfers between devices  24.2 us (20%)
  local copies, waits for them, and re-layouts  5.4 us (4%)
  between operations  1.69 us (1%)
    pallas_call x1, Pallas kernels, shards(): call(second_kernel, [(8, atoms), (atoms, 4 * CH), (ghosts, 4 * CH), (atom...  29.7 us
    ppermute x4, waiting for transfers between devices, exchange(): lax.ppermute(jnp.concatenate([up[2:3], x[6:7], down[2:3]]), 'gx', ring('g...  21.7 us
    ppermute x4, starting transfers between devices, exchange(): lax.ppermute(jnp.concatenate([x[0:1], x[3:4], x[5:6]]), 'gy', ring('gy',...  14.6 us
    pallas_call x1, Pallas kernels, shards(): call(third_kernel, [(8, atoms), (EXT, LANES)], [SMEM] * 2 + [VMEM] * 18,...  11.3 us
    ppermute x4, waiting for transfers between devices, exchange(): lax.ppermute(jnp.concatenate([x[2:3], x[4:5], x[7:8]]), 'gy', ring('gy', 1))  10 us
    pallas_call x1, Pallas kernels, shards(): call(first_kernel, [(atoms, 4 * CH), (ghosts, 4 * CH), (atoms, 4 * CH), (...  9.92 us
    ppermute x4, starting transfers between devices, exchange(): lax.ppermute(jnp.concatenate([up[0:1], x[1:2], down[0:1]]), 'gx', ring('g...  5.31 us
    ppermute x4, waiting for transfers between devices, exchange(): lax.ppermute(jnp.concatenate([up[0:1], x[1:2], down[0:1]]), 'gx', ring('g...  4.91 us
  transfers between devices with their start and end apart: 16, of which 10 were waited for; matrix products, arithmetic and copies ran while one was open for 1% of the time, Pallas kernels for 0%

profile of v1, /device:TPU:6, one launch (start us, length us, event | category | flops | bytes accessed | tf_op | source)
XLA Modules:
  0.0 120.5 jit_solution(18008207950293438057)
XLA Ops:
  0.6 0.8 broadcast_in_dim_reshape.3.lists
  1.4 0.7 copy-done.2
  2.1 0.2 shard_map.131
  2.5 1.7 %collective-permute-start = (f32[3,4,32]{2,0,1:T(4,128)S(1)}, f32[3,4,32]{2,0,1:T(4,128)S(1)}, u32[]{:S(2)}, u32[]{:S(2)}) collective-permute-start(f32[3,4,32]{2,0,1:T(4,128)S(1)} %pad_maximum_fusion.9), channel_id=1, source_target_pairs={{0,1},{1,2},{2,3},{3,4},{4,5},{5,6},{6,7},{7,0},{8,9},{9,10},{10,1... | collective-permute-start | bytes 4616 | tf_op jit(solution)/shard_map/ppermute | solution.py:360
  4.2 2.6 %collective-permute-start.1 = (f32[3,4,32]{2,0,1:T(4,128)S(1)}, f32[3,4,32]{2,0,1:T(4,128)S(1)}, u32[]{:S(2)}, u32[]{:S(2)}) collective-permute-start(f32[3,4,32]{2,0,1:T(4,128)S(1)} %pad_maximum_fusion.10), channel_id=1, source_target_pairs={{0,7},{1,0},{2,1},{3,2},{4,3},{5,4},{6,5},{7,6},{8,15},{9,8},{10,9... | collective-permute-start | bytes 4616 | tf_op jit(solution)/shard_map/ppermute | solution.py:361
  7.0 1.4 %collective-permute-done = f32[3,4,32]{2,0,1:T(4,128)S(1)} collective-permute-done((f32[3,4,32]{2,0,1:T(4,128)S(1)}, f32[3,4,32]{2,0,1:T(4,128)S(1)}, u32[]{:S(2)}, u32[]{:S(2)}) %collective-permute-start) | collective-permute-done | bytes 1568 | tf_op jit(solution)/shard_map/ppermute | solution.py:360
  8.4 5.1 %collective-permute-start.3 = (f32[3,4,32]{2,0,1:T(4,128)S(1)}, f32[3,4,32]{2,0,1:T(4,128)S(1)}, u32[]{:S(2)}, u32[]{:S(2)}) collective-permute-start(f32[3,4,32]{2,0,1:T(4,128)S(1)} %pad_maximum_fusion.12), channel_id=1, source_target_pairs={{0,248},{8,0},{16,8},{24,16},{32,24},{40,32},{48,40},{56,48},{64,5... | collective-permute-start | bytes 4616 | tf_op jit(solution)/shard_map/ppermute | solution.py:362
  13.5 0.6 copy-done.8
  15.4 4.8 %collective-permute-done.2 = f32[3,4,32]{2,0,1:T(4,128)S(1)} collective-permute-done((f32[3,4,32]{2,0,1:T(4,128)S(1)}, f32[3,4,32]{2,0,1:T(4,128)S(1)}, u32[]{:S(2)}, u32[]{:S(2)}) %collective-permute-start.2) | collective-permute-done | bytes 1568 | tf_op jit(solution)/shard_map/ppermute | solution.py:363
  20.4 0.1 tile.10.xt
  20.5 0.5 copy-done.4
  21.0 9.9 %shard_map.132 = (f32[512,512]{1,0:T(8,128)S(1)}, f32[256,512]{1,0:T(8,128)S(1)}, f32[512,512]{1,0:T(8,128)S(1)}, f32[512,256]{1,0:T(8,128)S(1)}, f32[512,384]{1,0:T(8,128)S(1)}) custom-call(s32[64]{0:T(128)S(1)} %reshape.87.pairs, s32[1]{0:T(128)} %bitcast.76.count, s32[256]{0:T(256)S(1)} %reshape.90.lists, f32[4,24,128]{2,1,0:T(8,128)S(1)} %tile.10.xt, ...), custom_call_target="tpu_custom_call" | custom-call | tf_op jit(solution)/shard_map/pallas_call | solution.py:408
  31.0 0.6 collective-permute-start.4
  31.7 3.7 %collective-permute-start.5 = (f32[3,32,512]{2,1,0:T(8,128)S(1)}, f32[3,32,512]{2,1,0:T(8,128)S(1)}, u32[]{:S(2)}, u32[]{:S(2)}) collective-permute-start(f32[3,32,512]{2,1,0:T(8,128)S(1)} %pad_maximum_fusion.1), channel_id=1, source_target_pairs={{0,7},{1,0},{2,1},{3,2},{4,3},{5,4},{6,5},{7,6},{8,15},{9,8},{10,9... | collective-permute-start | bytes 589832 | tf_op jit(solution)/shard_map/ppermute | solution.py:361
  35.4 3.5 %collective-permute-done.4 = f32[3,32,512]{2,1,0:T(8,128)S(1)} collective-permute-done((f32[3,32,512]{2,1,0:T(8,128)S(1)}, f32[3,32,512]{2,1,0:T(8,128)S(1)}, u32[]{:S(2)}, u32[]{:S(2)}) %collective-permute-start.4) | collective-permute-done | bytes 196640 | tf_op jit(solution)/shard_map/ppermute | solution.py:360
  39.1 0.5 collective-permute-start.7
  39.8 2.5 %collective-permute-done.6 = f32[3,32,512]{2,1,0:T(8,128)S(1)} collective-permute-done((f32[3,32,512]{2,1,0:T(8,128)S(1)}, f32[3,32,512]{2,1,0:T(8,128)S(1)}, u32[]{:S(2)}, u32[]{:S(2)}) %collective-permute-start.6) | collective-permute-done | bytes 196640 | tf_op jit(solution)/shard_map/ppermute | solution.py:362
  42.2 5.7 %collective-permute-done.7 = f32[3,32,512]{2,1,0:T(8,128)S(1)} collective-permute-done((f32[3,32,512]{2,1,0:T(8,128)S(1)}, f32[3,32,512]{2,1,0:T(8,128)S(1)}, u32[]{:S(2)}, u32[]{:S(2)}) %collective-permute-start.7) | collective-permute-done | bytes 196640 | tf_op jit(solution)/shard_map/ppermute | solution.py:363
  47.9 0.7 copy-done.6
  48.6 29.7 %shard_map.133 = (f32[8,512]{1,0:T(8,128)S(1)}, f32[512,512]{1,0:T(8,128)S(1)}, f32[256,512]{1,0:T(8,128)S(1)}, f32[512,128]{1,0:T(8,128)S(1)}, f32[24,128]{1,0:T(8,128)S(1)}) custom-call(s32[64]{0:T(128)S(1)} %reshape.87.pairs, s32[1]{0:T(128)} %bitcast.77.count, f32[4,24,128]{2,1,0:T(8,128)S(1)} %tile.10.xt, f32[512,8]{1,0:T(8,128)S(1)} %bitcast.80, ...), custom_call_target="tpu_custom_call" | custom-call | tf_op jit(solution)/shard_map/pallas_call | solution.py:417
  78.5 4.2 %collective-permute-start.9 = (f32[3,32,512]{2,1,0:T(8,128)S(1)}, f32[3,32,512]{2,1,0:T(8,128)S(1)}, u32[]{:S(2)}, u32[]{:S(2)}) collective-permute-start(f32[3,32,512]{2,1,0:T(8,128)S(1)} %pad_maximum_fusion.5), channel_id=1, source_target_pairs={{0,7},{1,0},{2,1},{3,2},{4,3},{5,4},{6,5},{7,6},{8,15},{9,8},{10,9... | collective-permute-start | bytes 589832 | tf_op jit(solution)/shard_map/ppermute | solution.py:361
  82.7 3.5 %collective-permute-done.8 = f32[3,32,512]{2,1,0:T(8,128)S(1)} collective-permute-done((f32[3,32,512]{2,1,0:T(8,128)S(1)}, f32[3,32,512]{2,1,0:T(8,128)S(1)}, u32[]{:S(2)}, u32[]{:S(2)}) %collective-permute-start.8) | collective-permute-done | bytes 196640 | tf_op jit(solution)/shard_map/ppermute | solution.py:360
  86.4 0.7 collective-permute-start.11
  87.2 2.4 %collective-permute-done.10 = f32[3,32,512]{2,1,0:T(8,128)S(1)} collective-permute-done((f32[3,32,512]{2,1,0:T(8,128)S(1)}, f32[3,32,512]{2,1,0:T(8,128)S(1)}, u32[]{:S(2)}, u32[]{:S(2)}) %collective-permute-start.10) | collective-permute-done | bytes 196640 | tf_op jit(solution)/shard_map/ppermute | solution.py:362
  89.6 5.8 %collective-permute-done.11 = f32[3,32,512]{2,1,0:T(8,128)S(1)} collective-permute-done((f32[3,32,512]{2,1,0:T(8,128)S(1)}, f32[3,32,512]{2,1,0:T(8,128)S(1)}, u32[]{:S(2)}, u32[]{:S(2)}) %collective-permute-start.11) | collective-permute-done | bytes 196640 | tf_op jit(solution)/shard_map/ppermute | solution.py:363
  95.4 11.3 %shard_map.134 = (f32[8,512]{1,0:T(8,128)S(1)}, f32[24,128]{1,0:T(8,128)S(1)}) custom-call(s32[64]{0:T(128)S(1)} %reshape.87.pairs, s32[1]{0:T(128)} %bitcast.78.count, s32[1,256]{1,0:T(1,128)S(1)} %broadcast_in_dim_reshape.3.lists, f32[4,24,128]{2,1,0:T(8,128)S(1)} %tile.10.xt, f32[512,8]{1,0:T(8,128)S(1)} %bitcast.81, ...), custom_call_target="tpu_custom_call" | custom-call | tf_op jit(solution)/shard_map/pallas_call | solution.py:430
  106.9 4.1 %collective-permute-start.13 = (f32[3,1,128]{2,1,0:T(1,128)S(1)}, f32[3,1,128]{2,1,0:T(1,128)S(1)}, u32[]{:S(2)}, u32[]{:S(2)}) collective-permute-start(f32[3,1,128]{2,1,0:T(1,128)S(1)} %pad_maximum_fusion.14), channel_id=1, source_target_pairs={{0,7},{1,0},{2,1},{3,2},{4,3},{5,4},{6,5},{7,6},{8,15},{9,8},{10,9... | collective-permute-start | bytes 4616 | tf_op jit(solution)/shard_map/ppermute | solution.py:361
  111.0 1.5 %collective-permute-done.12 = f32[3,1,128]{2,1,0:T(1,128)S(1)} collective-permute-done((f32[3,1,128]{2,1,0:T(1,128)S(1)}, f32[3,1,128]{2,1,0:T(1,128)S(1)}, u32[]{:S(2)}, u32[]{:S(2)}) %collective-permute-start.12) | collective-permute-done | bytes 1568 | tf_op jit(solution)/shard_map/ppermute | solution.py:360
  112.7 0.5 collective-permute-start.14
  113.2 0.6 slice.332
  113.9 5.4 %collective-permute-done.14 = f32[3,1,128]{2,1,0:T(1,128)S(1)} collective-permute-done((f32[3,1,128]{2,1,0:T(1,128)S(1)}, f32[3,1,128]{2,1,0:T(1,128)S(1)}, u32[]{:S(2)}, u32[]{:S(2)}) %collective-permute-start.14) | collective-permute-done | bytes 1568 | tf_op jit(solution)/shard_map/ppermute | solution.py:363
  119.6 0.9 shard_map.135
  (88 shorter events, 2.4 us)
Async XLA Ops:
  0.6 0.8 copy-start.5
  1.4 0.7 copy-start.2
  2.5 5.8 %collective-permute-start = (f32[3,4,32]{2,0,1:T(4,128)S(1)}, f32[3,4,32]{2,0,1:T(4,128)S(1)}, u32[]{:S(2)}, u32[]{:S(2)}) collective-permute-start(f32[3,4,32]{2,0,1:T(4,128)S(1)} %pad_maximum_fusion.9), channel_id=1, source_target_pairs={{0,1},{1,2},{2,3},{3,4},{4,5},{5,6},{6,7},{7,0},{8,9},{9,10},{10,1... | collective-permute-start | bytes 4616 | tf_op jit(solution)/shard_map/ppermute | solution.py:360
  4.1 2.7 %copy-start.3 = (f32[3,512]{1,0:T(4,128)S(1)}, f32[3,512]{1,0:T(4,128)}, u32[]{:S(2)}) copy-start(f32[3,512]{1,0:T(4,128)} %pos.1) | copy-start | bytes 18436
  4.2 4.2 %collective-permute-start.1 = (f32[3,4,32]{2,0,1:T(4,128)S(1)}, f32[3,4,32]{2,0,1:T(4,128)S(1)}, u32[]{:S(2)}, u32[]{:S(2)}) collective-permute-start(f32[3,4,32]{2,0,1:T(4,128)S(1)} %pad_maximum_fusion.10), channel_id=1, source_target_pairs={{0,7},{1,0},{2,1},{3,2},{4,3},{5,4},{6,5},{7,6},{8,15},{9,8},{10,9... | collective-permute-start | bytes 4616 | tf_op jit(solution)/shard_map/ppermute | solution.py:361
  8.4 7.0 %collective-permute-start.3 = (f32[3,4,32]{2,0,1:T(4,128)S(1)}, f32[3,4,32]{2,0,1:T(4,128)S(1)}, u32[]{:S(2)}, u32[]{:S(2)}) collective-permute-start(f32[3,4,32]{2,0,1:T(4,128)S(1)} %pad_maximum_fusion.12), channel_id=1, source_target_pairs={{0,248},{8,0},{16,8},{24,16},{32,24},{40,32},{48,40},{56,48},{64,5... | collective-permute-start | bytes 4616 | tf_op jit(solution)/shard_map/ppermute | solution.py:362
  13.4 0.7 copy-start.8
  13.4 0.7 copy-start.7
  13.5 6.8 %collective-permute-start.2 = (f32[3,4,32]{2,0,1:T(4,128)S(1)}, f32[3,4,32]{2,0,1:T(4,128)S(1)}, u32[]{:S(2)}, u32[]{:S(2)}) collective-permute-start(f32[3,4,32]{2,0,1:T(4,128)S(1)} %pad_maximum_fusion.11), channel_id=1, source_target_pairs={{0,8},{8,16},{16,24},{24,32},{32,40},{40,48},{48,56},{56,64},{64,7... | collective-permute-start | bytes 4616 | tf_op jit(solution)/shard_map/ppermute | solution.py:363
  14.4 0.7 copy-start.11
  15.2 5.0 %copy-start.10 = (f32[8,4]{0,1:T(4,128)S(1)}, f32[8,4]{0,1:T(4,128)}, u32[]{:S(2)}) copy-start(f32[8,4]{0,1:T(4,128)} %constant.13) | copy-start | bytes 388
  15.4 5.1 %copy-start = (f32[5,128,128]{2,1,0:T(8,128)S(1)}, f32[5,128,128]{2,1,0:T(8,128)}, u32[]{:S(2)}) copy-start(f32[5,128,128]{2,1,0:T(8,128)} %mix.5) | copy-start | bytes 983044
  20.4 0.7 copy-start.4
  31.0 7.9 %collective-permute-start.4 = (f32[3,32,512]{2,1,0:T(8,128)S(1)}, f32[3,32,512]{2,1,0:T(8,128)S(1)}, u32[]{:S(2)}, u32[]{:S(2)}) collective-permute-start(f32[3,32,512]{2,1,0:T(8,128)S(1)} %pad_maximum_fusion), channel_id=1, source_target_pairs={{0,1},{1,2},{2,3},{3,4},{4,5},{5,6},{6,7},{7,0},{8,9},{9,10},{10,1... | collective-permute-start | bytes 589832 | tf_op jit(solution)/shard_map/ppermute | solution.py:360
  31.7 7.2 %collective-permute-start.5 = (f32[3,32,512]{2,1,0:T(8,128)S(1)}, f32[3,32,512]{2,1,0:T(8,128)S(1)}, u32[]{:S(2)}, u32[]{:S(2)}) collective-permute-start(f32[3,32,512]{2,1,0:T(8,128)S(1)} %pad_maximum_fusion.1), channel_id=1, source_target_pairs={{0,7},{1,0},{2,1},{3,2},{4,3},{5,4},{6,5},{7,6},{8,15},{9,8},{10,9... | collective-permute-start | bytes 589832 | tf_op jit(solution)/shard_map/ppermute | solution.py:361
  39.0 3.3 %collective-permute-start.6 = (f32[3,32,512]{2,1,0:T(8,128)S(1)}, f32[3,32,512]{2,1,0:T(8,128)S(1)}, u32[]{:S(2)}, u32[]{:S(2)}) collective-permute-start(f32[3,32,512]{2,1,0:T(8,128)S(1)} %pad_maximum_fusion.2), channel_id=1, source_target_pairs={{0,248},{8,0},{16,8},{24,16},{32,24},{40,32},{48,40},{56,48},{64,5... | collective-permute-start | bytes 589832 | tf_op jit(solution)/shard_map/ppermute | solution.py:362
  39.1 0.7 copy-start.9
  39.1 8.8 %copy-start.1 = (f32[2,128,128]{2,1,0:T(8,128)S(1)}, f32[2,128,128]{2,1,0:T(8,128)}, u32[]{:S(2)}) copy-start(f32[2,128,128]{2,1,0:T(8,128)} %mix_two.1) | copy-start | bytes 393220
  39.1 8.8 %collective-permute-start.7 = (f32[3,32,512]{2,1,0:T(8,128)S(1)}, f32[3,32,512]{2,1,0:T(8,128)S(1)}, u32[]{:S(2)}, u32[]{:S(2)}) collective-permute-start(f32[3,32,512]{2,1,0:T(8,128)S(1)} %pad_maximum_fusion.3), channel_id=1, source_target_pairs={{0,8},{8,16},{16,24},{24,32},{32,40},{40,48},{48,56},{56,64},{64,7... | collective-permute-start | bytes 589832 | tf_op jit(solution)/shard_map/ppermute | solution.py:363
  47.9 0.7 copy-start.6
  78.4 7.9 %collective-permute-start.8 = (f32[3,32,512]{2,1,0:T(8,128)S(1)}, f32[3,32,512]{2,1,0:T(8,128)S(1)}, u32[]{:S(2)}, u32[]{:S(2)}) collective-permute-start(f32[3,32,512]{2,1,0:T(8,128)S(1)} %pad_maximum_fusion.4), channel_id=1, source_target_pairs={{0,1},{1,2},{2,3},{3,4},{4,5},{5,6},{6,7},{7,0},{8,9},{9,10},{10,1... | collective-permute-start | bytes 589832 | tf_op jit(solution)/shard_map/ppermute | solution.py:360
  78.5 7.8 %collective-permute-start.9 = (f32[3,32,512]{2,1,0:T(8,128)S(1)}, f32[3,32,512]{2,1,0:T(8,128)S(1)}, u32[]{:S(2)}, u32[]{:S(2)}) collective-permute-start(f32[3,32,512]{2,1,0:T(8,128)S(1)} %pad_maximum_fusion.5), channel_id=1, source_target_pairs={{0,7},{1,0},{2,1},{3,2},{4,3},{5,4},{6,5},{7,6},{8,15},{9,8},{10,9... | collective-permute-start | bytes 589832 | tf_op jit(solution)/shard_map/ppermute | solution.py:361
  86.3 3.3 %collective-permute-start.10 = (f32[3,32,512]{2,1,0:T(8,128)S(1)}, f32[3,32,512]{2,1,0:T(8,128)S(1)}, u32[]{:S(2)}, u32[]{:S(2)}) collective-permute-start(f32[3,32,512]{2,1,0:T(8,128)S(1)} %pad_maximum_fusion.6), channel_id=1, source_target_pairs={{0,248},{8,0},{16,8},{24,16},{32,24},{40,32},{48,40},{56,48},{64,5... | collective-permute-start | bytes 589832 | tf_op jit(solution)/shard_map/ppermute | solution.py:362
  86.4 9.0 %collective-permute-start.11 = (f32[3,32,512]{2,1,0:T(8,128)S(1)}, f32[3,32,512]{2,1,0:T(8,128)S(1)}, u32[]{:S(2)}, u32[]{:S(2)}) collective-permute-start(f32[3,32,512]{2,1,0:T(8,128)S(1)} %pad_maximum_fusion.7), channel_id=1, source_target_pairs={{0,8},{8,16},{16,24},{24,32},{32,40},{40,48},{48,56},{56,64},{64,7... | collective-permute-start | bytes 589832 | tf_op jit(solution)/shard_map/ppermute | solution.py:363
  106.8 5.8 %collective-permute-start.12 = (f32[3,1,128]{2,1,0:T(1,128)S(1)}, f32[3,1,128]{2,1,0:T(1,128)S(1)}, u32[]{:S(2)}, u32[]{:S(2)}) collective-permute-start(f32[3,1,128]{2,1,0:T(1,128)S(1)} %pad_maximum_fusion.13), channel_id=1, source_target_pairs={{0,1},{1,2},{2,3},{3,4},{4,5},{5,6},{6,7},{7,0},{8,9},{9,10},{10,1... | collective-permute-start | bytes 4616 | tf_op jit(solution)/shard_map/ppermute | solution.py:360
  106.9 5.7 %collective-permute-start.13 = (f32[3,1,128]{2,1,0:T(1,128)S(1)}, f32[3,1,128]{2,1,0:T(1,128)S(1)}, u32[]{:S(2)}, u32[]{:S(2)}) collective-permute-start(f32[3,1,128]{2,1,0:T(1,128)S(1)} %pad_maximum_fusion.14), channel_id=1, source_target_pairs={{0,7},{1,0},{2,1},{3,2},{4,3},{5,4},{6,5},{7,6},{8,15},{9,8},{10,9... | collective-permute-start | bytes 4616 | tf_op jit(solution)/shard_map/ppermute | solution.py:361
  112.6 1.4 %collective-permute-start.15 = (f32[3,1,128]{2,1,0:T(1,128)S(1)}, f32[3,1,128]{2,1,0:T(1,128)S(1)}, u32[]{:S(2)}, u32[]{:S(2)}) collective-permute-start(f32[3,1,128]{2,1,0:T(1,128)S(1)} %pad_maximum_fusion.16), channel_id=1, source_target_pairs={{0,248},{8,0},{16,8},{24,16},{32,24},{40,32},{48,40},{56,48},{64,5... | collective-permute-start | bytes 4616 | tf_op jit(solution)/shard_map/ppermute | solution.py:362
  112.7 6.7 %collective-permute-start.14 = (f32[3,1,128]{2,1,0:T(1,128)S(1)}, f32[3,1,128]{2,1,0:T(1,128)S(1)}, u32[]{:S(2)}, u32[]{:S(2)}) collective-permute-start(f32[3,1,128]{2,1,0:T(1,128)S(1)} %pad_maximum_fusion.15), channel_id=1, source_target_pairs={{0,8},{8,16},{16,24},{24,32},{32,40},{40,48},{48,56},{56,64},{64,7... | collective-permute-start | bytes 4616 | tf_op jit(solution)/shard_map/ppermute | solution.py:363

commit v2 on v1

v2 whole, which is shorter than its diff:
```python
import functools

import jax
import jax.numpy as jnp
import numpy as np
from jax import lax
from jax.experimental import pallas as pl
from jax.experimental.pallas import tpu as pltpu
from jax.sharding import PartitionSpec as P

NB = 8
CELL = 32
CH = 128
LANES = 128
OWN = 16
CUT2 = 25.0
STEPS_X = np.array([-1, -1, -1, 0, 0, 1, 1, 1])
STEPS_Y = np.array([-1, 0, 1, -1, 1, -1, 0, 1])
F32 = jnp.float32
BF16 = jnp.bfloat16
VMEM = pltpu.VMEM
SMEM = pltpu.SMEM
PARAMS = pltpu.CompilerParams(vmem_limit_bytes=32 * 1024 * 1024)
CHUNK = 128
HIST = 256
FEAT = 512
SLOTS = 32
UNROLL_OWN = 8
UNROLL_GHOST = 4
UP = (2, 4, 7)
DOWN = (0, 3, 5)
MID = (1, 6)

NN = (((1,), (0,)), ((), ()))
NT = (((1,), (1,)), ((), ()))
TN = (((0,), (0,)), ((), ()))


def split(x):
    hi = x.astype(BF16)
    return hi, (x - hi.astype(F32)).astype(BF16)


def mm(a, b, dims):
    return lax.dot_general(a, b, dims, preferred_element_type=F32)


def mm3(a, b, dims):
    (ah, al), (bh, bl) = a, b
    return mm(ah, bh, dims) + (mm(ah, bl, dims) + mm(al, bh, dims))


def mm3_deep(a, b, dims):
    (ah, al), (bh, bl) = a, b
    axis = dims[0][1][0]
    return mm(jnp.concatenate([ah, al], axis=1), jnp.concatenate([bh, bh], axis=axis), dims) + mm(ah, bl, dims)


def mm3_wide(a, b, dims):
    (ah, al), (bh, bl) = a, b
    width = 128
    out = mm(ah, jnp.concatenate([bh, bl], axis=1 - dims[0][1][0]), dims)
    return out[:, :width] + (out[:, width:] + mm(al, bh, dims))


def mm3_full(a, b, dims):
    (ah, al), (bh, bl) = a, b
    axis = dims[0][1][0]
    top = jnp.concatenate([bh, bh], axis=axis)
    low = jnp.concatenate([bl, jnp.zeros_like(bl)], axis=axis)
    out = mm(jnp.concatenate([ah, al], axis=1), jnp.concatenate([top, low], axis=1 - axis), dims)
    return out[:, :128] + out[:, 128:]


def mm3_turned(a, b):
    (ah, al), (bh, bl) = a, b
    out = mm(jnp.concatenate([ah, al], axis=1), bh, TN)
    width = ah.shape[1]
    return out[:width] + (out[width:] + mm(ah, bl, TN))


def iota(shape, dim):
    return lax.broadcasted_iota(jnp.int32, shape, dim)


def cell_rows(c):
    return pl.ds(pl.multiple_of(c * CELL, CELL), CELL)


def chunk_rows(i):
    return pl.ds(pl.multiple_of(i * CHUNK, CHUNK), CHUNK)


def geometry(r, c, keep, prc, xt):
    own = prc[cell_rows(r), :]
    far = xt[c]
    vec = [far[t + 1 : t + 2, :] - own[:, t : t + 1] for t in range(3)]
    sq = vec[0] * vec[0] + vec[1] * vec[1] + vec[2] * vec[2]
    group = iota((CELL, LANES), 1) // CELL
    edge = jnp.maximum(1.0 - sq * (1.0 / CUT2), 0.0)
    slope = edge * keep
    vk = jnp.where(group == 0, 1.0, jnp.where(group == 1, vec[0], jnp.where(group == 2, vec[1], vec[2])))
    scaled = sq * ((NB - 1) / CUT2)
    return edge * slope, slope, scaled, vk


def own_keep(r, c, weight):
    lane = iota((CELL, LANES), 1)
    row = iota((CELL, LANES), 0)
    return jnp.where(jnp.logical_and(lane % CELL == row, r == c), 0.0, weight)


def basis(scaled, n):
    off = scaled - float(n)
    return jnp.exp(-(off * off))


def pair_parts(env, scaled, vk):
    m = env * vk
    return [m * basis(scaled, n) for n in range(NB)]


def pair_force(deriv, env, slope, scaled, vk):
    total = None
    moment = None
    for n in range(NB):
        term = deriv[n] * basis(scaled, n)
        total = term if n == 0 else total + term
        if n == 1:
            moment = term
        elif n > 1:
            moment = moment + float(n) * term
    spacing = CUT2 / (NB - 1)
    by_sq = (-2.0 / CUT2) * slope * total - (2.0 / spacing) * env * (scaled * total - moment)
    by_sq = by_sq * vk
    by_sq = by_sq + pltpu.roll(by_sq, 64, 1)
    by_sq = by_sq + pltpu.roll(by_sq, 32, 1)
    return env * total + 2.0 * vk * by_sq


def add_force(force, r, c, recv, send):
    recv[cell_rows(r), :] += force
    send[pl.ds(c, 1), :] += jnp.sum(force, axis=0, keepdims=True)


def species_tile(c, xt):
    row = iota((4 * NB, LANES), 0)
    lane = iota((4 * NB, LANES), 1)
    kind = xt[c][0:1, :].astype(jnp.int32)
    hit = jnp.logical_and(kind == row % NB, lane // CELL == row // NB)
    hot = jnp.where(hit, 1.0, 0.0).astype(BF16)
    zero = jnp.zeros_like(hot)
    return jnp.concatenate(
        [jnp.concatenate([hot if j == k else zero for k in range(4)], axis=1) for j in range(4)], axis=0
    )


def add_histogram(r, c, keep, prc, xt, hist):
    env, slope, scaled, vk = geometry(r, c, keep, prc, xt)
    parts = pair_parts(env, scaled, vk)
    wide = jnp.concatenate([jnp.concatenate(parts[4 * h : 4 * h + 4], axis=1) for h in range(2)], axis=0)
    out = mm(jnp.concatenate(split(wide), axis=0), species_tile(c, xt), NT)
    out = out[: 2 * CELL] + out[2 * CELL :]
    hist[cell_rows(r), :] += jnp.concatenate([out[:CELL], out[CELL:]], axis=1)


def first_deriv(r, c, xt, quad):
    q = quad[cell_rows(r), :]
    q = jnp.concatenate([q[:, :LANES], q[:, LANES:]], axis=0)
    out = mm(jnp.concatenate(split(q), axis=0), species_tile(c, xt), NN)
    out = out[: 2 * CELL] + out[2 * CELL :]
    return [out[(n // 4) * CELL : (n // 4 + 1) * CELL, (n % 4) * LANES : (n % 4 + 1) * LANES] for n in range(NB)]


def cell_features(table, c):
    hi, lo = split(table[cell_rows(c), :])
    zero = jnp.zeros((CELL, CH), BF16)

    def lay(x):
        rows = [jnp.concatenate([x[:, :CH], zero], axis=1)]
        rows += [jnp.concatenate([zero, x[:, (t + 1) * CH : (t + 2) * CH]], axis=1) for t in range(3)]
        return jnp.concatenate(rows, axis=0)

    return lay(hi), lay(lo)


def spread(g, radial):
    both = [
        jnp.concatenate([g * radial[0, n : n + 1, :], g * radial[1, n : n + 1, :]], axis=1) for n in range(NB)
    ]
    return split(jnp.concatenate(both, axis=0))


def add_forward(r, c, keep, prc, xt, table, radial, acc):
    env, slope, scaled, vk = geometry(r, c, keep, prc, xt)
    tile = split(jnp.concatenate(pair_parts(env, scaled, vk), axis=0))
    prod = mm3_deep(tile, cell_features(table, c), NN)
    part = None
    for n in range(NB):
        rows = prod[n * CELL : (n + 1) * CELL]
        term = rows[:, :CH] * radial[0, n : n + 1, :] + rows[:, CH:] * radial[1, n : n + 1, :]
        part = term if n == 0 else part + term
    acc[cell_rows(r), :] += part


def add_feature_grad(r, c, keep, prc, xt, grad_acc, radial, grad_table):
    env, slope, scaled, vk = geometry(r, c, keep, prc, xt)
    tile = split(jnp.concatenate(pair_parts(env, scaled, vk), axis=0))
    gf = mm3_turned(tile, spread(grad_acc[cell_rows(r), :], radial))
    grad_table[cell_rows(c), :] += jnp.concatenate(
        [gf[0:CELL, :CH]] + [gf[(t + 1) * CELL : (t + 2) * CELL, CH:] for t in range(3)], axis=1
    )


def second_deriv(r, c, grad_acc, radial, table):
    out = mm3_wide(spread(grad_acc[cell_rows(r), :], radial), cell_features(table, c), NT)
    return [out[n * CELL : (n + 1) * CELL] for n in range(NB)]


def for_blocks(plan, unroll, body):
    count = plan[2 * SLOTS]

    def step(i, carry):
        for k in range(unroll):
            slot = i * unroll + k
            body(plan[2 * slot], plan[2 * slot + 1], jnp.where(slot < count, 1.0, 0.0).astype(F32))
        return carry

    lax.fori_loop(0, (count + unroll - 1) // unroll, step, 0)


def species_weights(embed, radial):
    zero = jnp.zeros((NB, CH), F32)
    rows = []
    for n in range(NB):
        for k in range(4):
            part = embed * radial[min(k, 1), n : n + 1, :]
            rows.append(jnp.concatenate([part if j == k else zero for j in range(4)], axis=1))
    return split(jnp.concatenate(rows, axis=0))


def tile_group(x, k):
    x = jnp.where(iota(x.shape, 1) // CELL == k, x, 0.0)
    x = x + pltpu.roll(x, 64, 1)
    return x + pltpu.roll(x, 32, 1)


def store_pieces(pieces, up, down, mid):
    for out, order in ((up, UP), (down, DOWN), (mid, MID)):
        size = pieces[0].shape[0]
        for k, p in enumerate(order):
            out[k * size : (k + 1) * size, :] = pieces[p]


def arrived(left, right, up, down, size):
    at = lambda x, k: x[k * size : (k + 1) * size, :]
    return [at(right, 0), at(right, 1), at(right, 2), at(up, 1), at(down, 1), at(left, 0), at(left, 1), at(left, 2)]


def pack_kernel(pos_in, species_in, lists_in, up, down, mid, table_out, row_out, pos, species, lists, sems):
    copies = [
        pltpu.make_async_copy(src, dst, sems.at[k])
        for k, (src, dst) in enumerate(((pos_in, pos), (species_in, species), (lists_in, lists)))
    ]
    for copy in copies:
        copy.start()
    for copy in copies:
        copy.wait()
    kinds = species[...].astype(F32)
    table = jnp.concatenate([kinds, pos[...], jnp.zeros((4, kinds.shape[1]), F32)], axis=0)
    table_out[...] = table
    hi = table.astype(BF16)
    rest = table - hi.astype(F32)
    mid_part = rest.astype(BF16)
    low = (rest - mid_part.astype(F32)).astype(BF16)
    row = jnp.concatenate([lists[p : p + 1, :] for p in range(8)], axis=1)
    row_out[...] = row.astype(F32)
    hot = jnp.where(iota((table.shape[1], row.shape[1]), 0) == row, 1.0, 0.0).astype(BF16)
    out = mm(hi, hot, NN) + mm(mid_part, hot, NN) + mm(low, hot, NN)
    pieces = [
        jnp.concatenate([out[k : k + 1, p * CELL : (p + 1) * CELL] for k in range(4)], axis=1) for p in range(8)
    ]
    store_pieces(pieces, up, down, mid)


def weight_kernel(
    table, embed, radial_one, mix_one, radial_two, mix_two, readout,
    w_hi, w_lo, mats, begins, radial, rows, xt, prc,
):
    w_hi[...], w_lo[...] = species_weights(embed[...], 0.5 * radial_one[...])
    for k, m in enumerate((mix_one[0], mix_one[4], mix_one[1], mix_one[3], mix_two[0])):
        mats[0, k * CH : (k + 1) * CH, :], mats[1, k * CH : (k + 1) * CH, :] = split(m)
    begins[0], begins[1] = split(mm3(split(embed[...]), split(mix_one[2]), NT))
    radial[...] = 0.5 * radial_two[...]
    both = readout[...]
    rows[0:1, :] = both[0:1, :] + mm3(split(both), split(mix_two[1]), NN)[1:2, :]
    rows[1:2, :] = both[1:2, :]
    t = table[...]
    for c in range(OWN):
        xt[c] = tile_group(t[:, (c // 4) * LANES : (c // 4 + 1) * LANES], c % 4)
    prc[...] = jnp.concatenate([t[1:4], t[0:1], t[4:8]], axis=0).T


def own_first_kernel(pairs, count, xt, prc, plan_own, plan_ghost, hist):
    def clear(i, carry):
        plan_own[i] = 0
        plan_ghost[i] = 0
        return carry

    lax.fori_loop(0, 2 * SLOTS, clear, 0)

    def sort(i, carry):
        n_own, n_ghost = carry
        r, c = pairs[0, i], pairs[1, i]
        mine = c < OWN

        @pl.when(mine)
        def _():
            plan_own[2 * n_own] = r
            plan_own[2 * n_own + 1] = c

        @pl.when(jnp.logical_not(mine))
        def _():
            plan_ghost[2 * n_ghost] = r
            plan_ghost[2 * n_ghost + 1] = c - OWN

        step = mine.astype(jnp.int32)
        return n_own + step, n_ghost + 1 - step

    n_own, n_ghost = lax.fori_loop(0, count[0, 0], sort, (jnp.int32(0), jnp.int32(0)))
    plan_own[2 * SLOTS] = n_own
    plan_ghost[2 * SLOTS] = n_ghost
    hist[...] = jnp.zeros_like(hist)

    def block(r, c, weight):
        add_histogram(r, c, own_keep(r, c, weight), prc, xt, hist)

    for_blocks(plan_own, UNROLL_OWN, block)


def ghost_first_kernel(
    side, plan, lists, left, right, up, down, prc, hist_own, hist, xt, send_up, send_down, send_mid
):
    rows = jnp.concatenate(arrived(left, right, up, down, 1), axis=0)
    for k in range(4):
        part = tile_group(rows, k)
        for p in range(8):
            shift = 0.0 if k in (0, 3) else float((STEPS_X, STEPS_Y)[k - 1][p] * side)
            xt[p, k : k + 1, :] = part[p : p + 1, :] + shift
    hist[...] = hist_own[...]

    def block(r, c, weight):
        add_histogram(r, c, weight, prc, xt, hist)

    for_blocks(plan, UNROLL_GHOST, block)

    for out, order in ((send_up, UP), (send_down, DOWN), (send_mid, MID)):
        for k, p in enumerate(order):

            def gather(i, carry):
                for j in range(8):
                    at = i * 8 + j
                    out[pl.ds(k * CELL + at, 1), :] = hist[pl.ds(lists[p, at], 1), :]
                return carry

            lax.fori_loop(0, CELL // 8, gather, 0)


def first_update(joined, kind, weights, begin, mix04, mix1, mix3):
    size = joined.shape[0]
    a = mm3(split(joined), weights, NN)
    a0 = a[:, :CH]
    a1 = [a[:, (t + 1) * CH : (t + 2) * CH] for t in range(3)]
    power = a1[0] * a1[0] + a1[1] * a1[1] + a1[2] * a1[2]
    both = mm3_deep(split(a0), mix04, NT)
    z0 = both[:, :CH] + mm3_full(split(power), mix1, NT)
    gate = jax.nn.sigmoid(both[:, CH:])
    hot = jnp.where(kind == iota((size, NB), 1), 1.0, 0.0).astype(BF16)
    own = mm(hot, begin[0], NN) + mm(hot, begin[1], NN)
    lift = mm3_full(split(jnp.concatenate(a1, axis=0)), mix3, NT)
    lift = jnp.concatenate([lift[t * size : (t + 1) * size] for t in range(3)], axis=1)
    feat = jnp.concatenate(
        [z0 * jax.nn.sigmoid(z0) + own, lift * jnp.concatenate([gate] * 3, axis=1)], axis=1
    )
    return feat, a, jnp.concatenate([z0, gate], axis=1), lift


def first_pullback(gs, gv, a, gates, lift, weights, mix04, mix1, mix3):
    size = gs.shape[0]
    z0, gate = gates[:, :CH], gates[:, CH:]
    sg = jax.nn.sigmoid(z0)
    dz0 = gs * (sg * (1.0 + z0 * (1.0 - sg)))
    y = [lift[:, t * CH : (t + 1) * CH] for t in range(3)]
    dgate = gv[0] * y[0] + gv[1] * y[1] + gv[2] * y[2]
    dz4 = dgate * gate * (1.0 - gate)
    da0 = mm3_wide(split(jnp.concatenate([dz0, dz4], axis=1)), mix04, NN)
    dpower = 2.0 * mm3_full(split(dz0), mix1, NN)
    dy = mm3_full(split(jnp.concatenate([v * gate for v in gv], axis=0)), mix3, NN)
    parts = [da0] + [
        dy[t * size : (t + 1) * size] + a[:, (t + 1) * CH : (t + 2) * CH] * dpower for t in range(3)
    ]
    return mm3(split(jnp.concatenate(parts, axis=1)), weights, NT)


def mat(mats, first, rows):
    return mats[0, first : first + rows, :], mats[1, first : first + rows, :]


def mixes(mats):
    return mat(mats, 0, 2 * CH), mat(mats, 2 * CH, CH), mat(mats, 3 * CH, CH)


def features(g):
    return g[:, :CH], [g[:, (t + 1) * CH : (t + 2) * CH] for t in range(3)]


def own_update_kernel(joined, prc, w_hi, w_lo, begins, mats, feat, acc, gates, lifted):
    begin = begins[0], begins[1]
    mix_all = mixes(mats)

    def chunk(i, carry):
        rows = chunk_rows(i)
        kind = prc[rows, :][:, 3:4].astype(jnp.int32)
        out = first_update(joined[rows, :], kind, (w_hi[...], w_lo[...]), begin, *mix_all)
        feat[rows, :], acc[rows, :], gates[rows, :], lifted[rows, :] = out
        return carry

    lax.fori_loop(0, feat.shape[0] // CHUNK, chunk, 0)


def own_second_kernel(plan, prc, xt, feat, radial, acc):
    acc[...] = jnp.zeros_like(acc)

    def block(r, c, weight):
        add_forward(r, c, own_keep(r, c, weight), prc, xt, feat, radial, acc)

    for_blocks(plan, UNROLL_OWN, block)


def ghost_second_kernel(
    plan, prc, xt, left, right, up, down, w_hi, w_lo, begins, mats, acc_own, radial, readout,
    acc, grad_acc, feat, send_up, send_down, send_mid,
    joined, lin, gates, lifted, grad_table,
):
    ghosts = feat.shape[0]
    for p, piece in enumerate(arrived(left, right, up, down, CELL)):
        joined[p * CELL : (p + 1) * CELL, :] = piece
    begin = begins[0], begins[1]
    mix_all = mixes(mats)
    acc[...] = acc_own[...]
    grad_table[...] = jnp.zeros_like(grad_table)
    kinds = jnp.concatenate([xt[p][0:8, 0:CELL] for p in range(8)], axis=1).T[:, 0:1].astype(jnp.int32)
    for i in range(ghosts // CHUNK):
        rows = pl.ds(i * CHUNK, CHUNK)
        kind = kinds[i * CHUNK : (i + 1) * CHUNK]
        out = first_update(joined[rows, :], kind, (w_hi[...], w_lo[...]), begin, *mix_all)
        feat[rows, :], lin[rows, :], gates[rows, :], lifted[rows, :] = out

    def forward(r, c, weight):
        add_forward(r, c, weight, prc, xt, feat, radial, acc)

    for_blocks(plan, UNROLL_GHOST, forward)

    mix0 = mat(mats, 4 * CH, CH)

    def chunk(i, carry):
        rows = chunk_rows(i)
        z = mm3_full(split(acc[rows, :]), mix0, NT)
        sg = jax.nn.sigmoid(z)
        gz = readout[1:2, :] * (sg * (1.0 + z * (1.0 - sg)))
        grad_acc[rows, :] = mm3_full(split(gz), mix0, NN)
        return carry

    lax.fori_loop(0, acc.shape[0] // CHUNK, chunk, 0)

    def backward(r, c, weight):
        add_feature_grad(r, c, weight, prc, xt, grad_acc, radial, grad_table)

    for_blocks(plan, UNROLL_GHOST, backward)

    pieces = []
    for i in range(ghosts // CHUNK):
        rows = pl.ds(i * CHUNK, CHUNK)
        gs, gv = features(grad_table[rows, :])
        q = first_pullback(gs, gv, lin[rows, :], gates[rows, :], lifted[rows, :], (w_hi[...], w_lo[...]), *mix_all)
        pieces += [q[k * CELL : (k + 1) * CELL] for k in range(CHUNK // CELL)]
    store_pieces(pieces, send_up, send_down, send_mid)


def own_grad_kernel(
    plan, prc, xt, grad_acc, radial, acc, feat, lin, gates, lifted, w_hi, w_lo, mats, readout,
    quad, energy,
    grad_table,
):
    atoms = feat.shape[0]
    grad_table[...] = jnp.zeros_like(grad_table)

    def block(r, c, weight):
        add_feature_grad(r, c, own_keep(r, c, weight), prc, xt, grad_acc, radial, grad_table)

    for_blocks(plan, UNROLL_OWN, block)
    mix_all = mixes(mats)
    mix0 = mat(mats, 4 * CH, CH)
    carry_w = readout[0:1, :]
    row8 = iota((8, CH), 0)
    first = split(jnp.where(row8 == 0, carry_w, 0.0))
    second = split(jnp.where(row8 == 0, readout[1:2, :], 0.0))
    for i in range(atoms // CHUNK):
        rows = pl.ds(i * CHUNK, CHUNK)
        z = mm3_full(split(acc[rows, :]), mix0, NT)
        s1 = feat[rows, :][:, :CH]
        e = mm3(first, split(s1), NT) + mm3(second, split(z * jax.nn.sigmoid(z)), NT)
        energy[:, i * CHUNK : (i + 1) * CHUNK] = e[0:1, :]

    def chunk(i, carry):
        rows = chunk_rows(i)
        gs, gv = features(grad_table[rows, :])
        quad[rows, :] = first_pullback(
            gs + carry_w, gv, lin[rows, :], gates[rows, :], lifted[rows, :], (w_hi[...], w_lo[...]), *mix_all
        )
        return carry

    lax.fori_loop(0, atoms // CHUNK, chunk, 0)


def ghost_force_kernel(plan, prc, xt, grad_acc, radial, feat, recv, send):
    recv[...] = jnp.zeros_like(recv)
    send[...] = jnp.zeros_like(send)

    def block(r, c, weight):
        env, slope, scaled, vk = geometry(r, c, weight, prc, xt)
        deriv = second_deriv(r, c, grad_acc, radial, feat)
        add_force(pair_force(deriv, env, slope, scaled, vk), r, c, recv, send)

    for_blocks(plan, UNROLL_GHOST, block)


def ghost_last_kernel(
    plan, lists, prc, xt, quad_own, left, right, up, down, recv_two, send_two,
    quad, recv, send_up, send_down, send_mid,
    back_hi, back_lo, send,
):
    for p, piece in enumerate(arrived(left, right, up, down, CELL)):
        hi, lo = split(piece)
        back_hi[p * CELL : (p + 1) * CELL, :] = hi
        back_lo[p * CELL : (p + 1) * CELL, :] = lo
    recv[...] = recv_two[...]
    send[...] = send_two[...]
    row = lists[...].astype(jnp.int32)

    def chunk(i, carry):
        rows = chunk_rows(i)
        hot = jnp.where(iota((CHUNK, row.shape[1]), 0) + i * CHUNK == row, 1.0, 0.0).astype(BF16)
        quad[rows, :] = quad_own[rows, :] + (mm(hot, back_hi[...], NN) + mm(hot, back_lo[...], NN))
        return carry

    lax.fori_loop(0, quad.shape[0] // CHUNK, chunk, 0)

    def block(r, c, weight):
        env, slope, scaled, vk = geometry(r, c, weight, prc, xt)
        add_force(pair_force(first_deriv(r, c, xt, quad), env, slope, scaled, vk), r, c, recv, send)

    for_blocks(plan, UNROLL_GHOST, block)
    store_pieces([send[p : p + 1, :] for p in range(8)], send_up, send_down, send_mid)


def by_axis(rows, count):
    lines = [
        jnp.concatenate([rows[p : p + 1, (t + 1) * CELL : (t + 2) * CELL] for p in range(count)], axis=1)
        for t in range(3)
    ]
    return lines


def own_force_kernel(plan, prc, xt, quad, grad_acc, radial, feat, recv_ghost, out, recv, send):
    recv[...] = recv_ghost[...]
    send[...] = jnp.zeros_like(send)

    def block(r, c, weight):
        env, slope, scaled, vk = geometry(r, c, own_keep(r, c, weight), prc, xt)
        one = first_deriv(r, c, xt, quad)
        two = second_deriv(r, c, grad_acc, radial, feat)
        deriv = [x + y for x, y in zip(one, two)]
        add_force(pair_force(deriv, env, slope, scaled, vk), r, c, recv, send)

    for_blocks(plan, UNROLL_OWN, block)
    pick = jnp.where(iota((8, LANES), 0) + 1 == iota((8, LANES), 1) // CELL, 1.0, 0.0).astype(BF16)
    hi, lo = split(recv[...])
    total = mm(pick, hi, NT) + mm(pick, lo, NT)
    out[...] = total[0:3, :] - jnp.concatenate(by_axis(send, OWN), axis=0)


def last_kernel(lists, left, right, up, down, partial, out):
    rows = jnp.concatenate(arrived(left, right, up, down, 1), axis=0)
    lines = by_axis(rows, 8)
    back = jnp.concatenate(lines + [jnp.zeros((5, lines[0].shape[1]), F32)], axis=0)
    hi, lo = split(back)
    row = lists[...].astype(jnp.int32)
    hot = jnp.where(iota((partial.shape[1], row.shape[1]), 0) == row, 1.0, 0.0).astype(BF16)
    ghost = mm(hi, hot, NT) + mm(lo, hot, NT)
    out[...] = partial[...] - ghost[0:3, :]


def ring(axis, step):
    count = lax.axis_size(axis)
    return [(i, (i + step) % count) for i in range(count)]


def exchange(up, down, mid, between=None):
    size = mid.shape[0] // 2
    part = lambda x, k: x[k * size : (k + 1) * size]
    up = lax.ppermute(up, "gy", ring("gy", 1))
    down = lax.ppermute(down, "gy", ring("gy", -1))
    if between is not None:
        up, down, between = lax.optimization_barrier((up, down, between))
    left = lax.ppermute(jnp.concatenate([part(up, 0), part(mid, 0), part(down, 0)]), "gx", ring("gx", -1))
    right = lax.ppermute(jnp.concatenate([part(up, 2), part(mid, 1), part(down, 2)]), "gx", ring("gx", 1))
    return (left, right, up, down), between


def call(kernel, outs, specs, scratch=()):
    spaces = [SMEM if s[1] == jnp.int32 else VMEM for s in outs]
    return pl.pallas_call(
        kernel,
        out_shape=[jax.ShapeDtypeStruct(*s) for s in outs],
        in_specs=[pl.BlockSpec(memory_space=s) for s in specs],
        out_specs=[pl.BlockSpec(memory_space=s) for s in spaces],
        scratch_shapes=list(scratch),
        compiler_params=PARAMS,
    )


def shards(
    positions, species, send_lists, cell_pairs, block_count,
    embed, radial_one, mix_one, radial_two, mix_two, readout,
):
    atoms = positions.shape[1]
    side = float((atoms * 10.0) ** (1.0 / 3.0))
    pairs = cell_pairs[0, 0].T
    lists = send_lists[0, 0]
    kinds = species[None, :]
    ghosts = lists.size
    f = lambda *shape: (shape, F32)
    b = lambda *shape: (shape, BF16)
    i = lambda *shape: (shape, jnp.int32)
    three = lambda size, width: [f(3 * size, width), f(3 * size, width), f(2 * size, width)]

    *sends, table, row = call(
        pack_kernel,
        three(1, LANES) + [f(8, atoms), f(1, ghosts)],
        [pl.ANY] * 3,
        [
            VMEM((3, atoms), F32),
            VMEM((1, atoms), jnp.int32),
            VMEM((8, CELL), jnp.int32),
            pltpu.SemaphoreType.DMA((3,)),
        ],
    )(positions, kinds, lists)
    ready = call(
        weight_kernel,
        [
            b(HIST, FEAT), b(HIST, FEAT), b(2, 5 * CH, CH), b(2, NB, CH), f(2, NB, CH), f(2, CH),
            f(OWN, 8, LANES), f(atoms, 8),
        ],
        [VMEM] * 7,
    )(table, embed, radial_one, mix_one, radial_two, mix_two, readout)
    moved, ready = exchange(*sends, ready)
    w_hi, w_lo, mats, begins, radial, rows, xt_own, prc = ready
    plan_own, plan_ghost, hist_own = call(
        own_first_kernel, [i(2 * SLOTS + 1), i(2 * SLOTS + 1), f(atoms, HIST)], [SMEM] * 2 + [VMEM] * 2
    )(pairs, block_count, xt_own, prc)
    hist, xt_ghost, *sends = call(
        functools.partial(ghost_first_kernel, side),
        [f(atoms, HIST), f(8, 8, LANES)] + three(CELL, HIST),
        [SMEM] * 2 + [VMEM] * 6,
    )(plan_ghost, lists, *moved, prc, hist_own)

    own = call(
        own_update_kernel, [f(atoms, FEAT), f(atoms, FEAT), f(atoms, 2 * CH), f(atoms, 3 * CH)], [VMEM] * 6
    )(hist, prc, w_hi, w_lo, begins, mats)
    moved, own = exchange(*sends, own)
    feat, lin, gates, lifted = own
    (acc_own,) = call(own_second_kernel, [f(atoms, CH)], [SMEM] + [VMEM] * 4)(
        plan_own, prc, xt_own, feat, radial
    )
    acc, grad_acc, feat_ghost, *sends = call(
        ghost_second_kernel,
        [f(atoms, CH), f(atoms, CH), f(ghosts, FEAT)] + three(CELL, HIST),
        [SMEM] + [VMEM] * 13,
        [
            VMEM((ghosts, HIST), F32),
            VMEM((ghosts, FEAT), F32),
            VMEM((ghosts, 2 * CH), F32),
            VMEM((ghosts, 3 * CH), F32),
            VMEM((ghosts, FEAT), F32),
        ],
    )(plan_ghost, prc, xt_ghost, *moved, w_hi, w_lo, begins, mats, acc_own, radial, rows)

    two = call(ghost_force_kernel, [f(atoms, LANES), f(8, LANES)], [SMEM] + [VMEM] * 5)(
        plan_ghost, prc, xt_ghost, grad_acc, radial, feat_ghost
    )
    moved, two = exchange(*sends, two)
    recv_two, send_two = two
    quad_own, energy = call(
        own_grad_kernel, [f(atoms, HIST), f(1, atoms)], [SMEM] + [VMEM] * 13, [VMEM((atoms, FEAT), F32)]
    )(plan_own, prc, xt_own, grad_acc, radial, acc, feat, lin, gates, lifted, w_hi, w_lo, mats, rows)
    quad, recv, *sends = call(
        ghost_last_kernel,
        [f(atoms, HIST), f(atoms, LANES)] + three(1, LANES),
        [SMEM] + [VMEM] * 10,
        [VMEM((ghosts, HIST), BF16), VMEM((ghosts, HIST), BF16), VMEM((8, LANES), F32)],
    )(plan_ghost, row, prc, xt_ghost, quad_own, *moved, recv_two, send_two)

    moved, unused = exchange(*sends)
    (partial,) = call(
        own_force_kernel,
        [f(3, atoms)],
        [SMEM] + [VMEM] * 7,
        [VMEM((atoms, LANES), F32), VMEM((OWN, LANES), F32)],
    )(plan_own, prc, xt_own, quad, grad_acc, radial, feat, recv)
    (forces,) = call(last_kernel, [f(3, atoms)], [VMEM] * 6)(row, *moved, partial)
    return forces, energy[0]


def solution(mesh):
    both = P(("gx", "gy"))
    in_specs = (
        P(None, ("gx", "gy")),
        both,
        P("gx", "gy", None, None),
        P("gx", "gy", None, None),
        P("gx", "gy"),
    ) + (P(),) * 6
    out_specs = (P(None, ("gx", "gy")), both)
    return jax.shard_map(shards, mesh=mesh, in_specs=in_specs, out_specs=out_specs, check_vma=False)
```

time: 122 us -> 88.5 us (0.73)
  waiting for transfers between devices: 36.6 us -> 9.48 us
  Pallas kernels: 52.1 us -> 39.3 us
  starting transfers between devices: 24.2 us -> 31.3 us
    ppermute x16, waiting for transfers between devices: 36.6 us -> 9.48 us  [the longest x4 7.66 us: exchange(): lax.ppermute(jnp.concatenate([part(up, 2), part(mid, 1), part(down, 2)]),...]
    pallas_call x5 -> x12, Pallas kernels: 52.1 us -> 39.3 us  [the longest x1 7.59 us: shards(): call(ghost_second_kernel, [f(atoms, CH), f(atoms, CH), f(ghosts, FEAT)] +...]
    ppermute x16, starting transfers between devices: 24.2 us -> 31.3 us  [the longest x4 15 us: exchange(): down = lax.ppermute(down, 'gy', ring('gy', -1))]
    unnamed x25 -> x22, local copies, waits for them, and re-layouts: 2.74 us -> 5.28 us
  transfers between devices with their start and end apart: 16 -> 16, of which waited for: 10 -> 6; matrix products, arithmetic and copies ran while one was open for 1% -> 0% of each run, Pallas kernels for 0% -> 28%
where the time goes in v2:
time: 88.5 us; the launch traced here: 87.1 us
  Pallas kernels  39.3 us (44%)
  starting transfers between devices  31.3 us (35%)
  waiting for transfers between devices  9.48 us (11%)
  local copies, waits for them, and re-layouts  5.33 us (6%)
  between operations  1.58 us (2%)
    ppermute x4, starting transfers between devices, exchange(): down = lax.ppermute(down, 'gy', ring('gy', -1))  15 us
    ppermute x4, starting transfers between devices, exchange(): lax.ppermute(jnp.concatenate([part(up, 0), part(mid, 0), part(down, 0)]),...  13.4 us
    ppermute x4, waiting for transfers between devices, exchange(): lax.ppermute(jnp.concatenate([part(up, 2), part(mid, 1), part(down, 2)]),...  7.66 us
    pallas_call x1, Pallas kernels, shards(): call(ghost_second_kernel, [f(atoms, CH), f(atoms, CH), f(ghosts, FEAT)] +...  7.59 us
    pallas_call x1, Pallas kernels, shards(): call(own_grad_kernel, [f(atoms, HIST), f(1, atoms)], [SMEM] + [VMEM] * 13...  7.39 us
    unnamed x22, local copies, waits for them, and re-layouts  5.28 us
    pallas_call x1, Pallas kernels, shards(): call(own_force_kernel, [f(3, atoms)], [SMEM] + [VMEM] * 7, [VMEM((atoms,...  4.75 us
    pallas_call x1, Pallas kernels, shards(): call(own_first_kernel, [i(2 * SLOTS + 1), i(2 * SLOTS + 1), f(atoms, HIST...  4.03 us
  transfers between devices with their start and end apart: 16, of which 6 were waited for; matrix products, arithmetic and copies ran while one was open for 0% of the time, Pallas kernels for 28%

profile of v2, /device:TPU:6, one launch (start us, length us, event | category | flops | bytes accessed | tf_op | source)
XLA Modules:
  0.0 87.1 jit_solution(4781128277428955022)
XLA Ops:
  0.6 0.7 copy-done.8
  1.3 0.7 copy-done.2
  2.0 0.7 copy-done.6
  2.7 0.4 shard_map.122
  3.1 1.7 %collective-permute-start = (f32[3,128]{1,0:T(4,128)S(1)}, f32[3,128]{1,0:T(4,128)S(1)}, u32[]{:S(2)}, u32[]{:S(2)}) collective-permute-start(f32[3,128]{1,0:T(4,128)S(1)} %get-tuple-element.63), channel_id=1, source_target_pairs={{0,1},{1,2},{2,3},{3,4},{4,5},{5,6},{6,7},{7,0},{8,9},{9,10},{10,1... | collective-permute-start | bytes 4616 | tf_op jit(solution)/shard_map/ppermute | solution.py:612
  4.8 2.6 %collective-permute-start.1 = (f32[3,128]{1,0:T(4,128)S(1)}, f32[3,128]{1,0:T(4,128)S(1)}, u32[]{:S(2)}, u32[]{:S(2)}) collective-permute-start(f32[3,128]{1,0:T(4,128)S(1)} %get-tuple-element.64), channel_id=1, source_target_pairs={{0,7},{1,0},{2,1},{3,2},{4,3},{5,4},{6,5},{7,6},{8,15},{9,8},{10,9... | collective-permute-start | bytes 4616 | tf_op jit(solution)/shard_map/ppermute | solution.py:613
  7.4 0.7 copy-done.9
  8.0 1.0 %copy-done = f32[5,128,128]{2,1,0:T(8,128)S(1)} copy-done((f32[5,128,128]{2,1,0:T(8,128)S(1)}, f32[5,128,128]{2,1,0:T(8,128)}, u32[]{:S(2)}) %copy-start) | copy-done | bytes 327704
  9.0 0.9 %copy-done.1 = f32[2,128,128]{2,1,0:T(8,128)S(1)} copy-done((f32[2,128,128]{2,1,0:T(8,128)S(1)}, f32[2,128,128]{2,1,0:T(8,128)}, u32[]{:S(2)}) %copy-start.1) | copy-done | bytes 131096
  9.9 0.3 shard_map.123
  10.2 5.7 %collective-permute-start.2 = (f32[3,128]{1,0:T(4,128)S(1)}, f32[3,128]{1,0:T(4,128)S(1)}, u32[]{:S(2)}, u32[]{:S(2)}) collective-permute-start(f32[3,128]{1,0:T(4,128)S(1)} %pad_maximum_fusion.4), channel_id=1, source_target_pairs={{0,248},{8,0},{16,8},{24,16},{32,24},{40,32},{48,40},{56,48},{64,5... | collective-permute-start | bytes 4616 | tf_op jit(solution)/shard_map/ppermute | solution.py:616
  16.6 0.7 copy-done.10
  17.3 4.0 %shard_map.124 = (s32[65]{0:T(128)S(1)}, s32[65]{0:T(128)S(1)}, f32[512,256]{1,0:T(8,128)S(1)}) custom-call(s32[2,32]{1,0:T(2,128)S(1)} %bitcast.9, s32[1,1]{1,0:T(1,128)S(6)} %copy.13.count, f32[16,8,128]{2,1,0:T(8,128)S(1)} %get-tuple-element.74.xt, f32[512,8]{1,0:T(8,128)S(1)} %get-tuple-element.75.prc), custom_call_target="tpu_custom_call" | custom-call | tf_op jit(solution)/shard_map/pallas_call | solution.py:669
  21.4 1.2 %collective-permute-done.3.right = f32[3,128]{1,0:T(4,128)S(1)} collective-permute-done((f32[3,128]{1,0:T(4,128)S(1)}, f32[3,128]{1,0:T(4,128)S(1)}, u32[]{:S(2)}, u32[]{:S(2)}) %collective-permute-start.3) | collective-permute-done | bytes 1568 | tf_op jit(solution)/shard_map/ppermute | solution.py:617
  22.6 3.3 %shard_map.125 = (f32[512,256]{1,0:T(8,128)S(1)}, f32[8,8,128]{2,1,0:T(8,128)S(1)}, f32[96,256]{1,0:T(8,128)S(1)}, f32[96,256]{1,0:T(8,128)S(1)}, f32[64,256]{1,0:T(8,128)S(1)}) custom-call(s32[65]{0:T(128)S(1)} %get-tuple-element.76.plan, s32[8,32]{1,0:T(8,128)S(1)} %bitcast.7, f32[3,128]{1,0:T(4,128)S(1)} %collective-permute-done.2.left, ...), custom_call_target="tpu_custom_call" | custom-call | tf_op jit(solution)/shard_map/pallas_call | solution.py:672
  26.0 4.1 %collective-permute-start.5 = (f32[96,256]{1,0:T(8,128)S(1)}, f32[96,256]{1,0:T(8,128)S(1)}, u32[]{:S(2)}, u32[]{:S(2)}) collective-permute-start(f32[96,256]{1,0:T(8,128)S(1)} %get-tuple-element.84), channel_id=1, source_target_pairs={{0,7},{1,0},{2,1},{3,2},{4,3},{5,4},{6,5},{7,6},{8,15},{9,8},{10,9... | collective-permute-start | bytes 294920 | tf_op jit(solution)/shard_map/ppermute | solution.py:613
  30.1 2.3 %shard_map.126 = (f32[512,512]{1,0:T(8,128)S(1)}, f32[512,512]{1,0:T(8,128)S(1)}, f32[512,256]{1,0:T(8,128)S(1)}, f32[512,384]{1,0:T(8,128)S(1)}) custom-call(f32[512,256]{1,0:T(8,128)S(1)} %get-tuple-element.85.joined, f32[512,8]{1,0:T(8,128)S(1)} %get-tuple-element.75.prc, bf16[256,512]{1,0:T(8,128)(2,1)S(1)} %get-tuple-element.86.w_hi, ...), custom_call_target="tpu_custom_call" | custom-call | tf_op jit(solution)/shard_map/pallas_call | solution.py:678
  32.8 3.0 %collective-permute-start.6 = (f32[96,256]{1,0:T(8,128)S(1)}, f32[96,256]{1,0:T(8,128)S(1)}, u32[]{:S(2)}, u32[]{:S(2)}) collective-permute-start(f32[96,256]{1,0:T(8,128)S(1)} %pad_maximum_fusion), channel_id=1, source_target_pairs={{0,248},{8,0},{16,8},{24,16},{32,24},{40,32},{48,40},{56,48},{64,5... | collective-permute-start | bytes 294920 | tf_op jit(solution)/shard_map/ppermute | solution.py:616
  35.8 3.1 %shard_map.127.acc_own = f32[512,128]{1,0:T(8,128)S(1)} custom-call(s32[65]{0:T(128)S(1)} %get-tuple-element.82.plan, f32[512,8]{1,0:T(8,128)S(1)} %get-tuple-element.75.prc, f32[16,8,128]{2,1,0:T(8,128)S(1)} %get-tuple-element.74.xt, f32[512,512]{1,0:T(8,128)S(1)} %get-tuple-element.97.feat, f32[2,8,128]{2,1,0:T(8,128)S(1)} %get-tuple-element.98.radial), custom_call_target="tpu_custom_call" | custom-call | tf_op jit(solution)/shard_map/pallas_call | solution.py:683
  38.9 4.6 %collective-permute-done.7.right = f32[96,256]{1,0:T(8,128)S(1)} collective-permute-done((f32[96,256]{1,0:T(8,128)S(1)}, f32[96,256]{1,0:T(8,128)S(1)}, u32[]{:S(2)}, u32[]{:S(2)}) %collective-permute-start.7) | collective-permute-done | bytes 98336 | tf_op jit(solution)/shard_map/ppermute | solution.py:617
  43.5 7.6 %shard_map.128 = (f32[512,128]{1,0:T(8,128)S(1)}, f32[512,128]{1,0:T(8,128)S(1)}, f32[256,512]{1,0:T(8,128)S(1)}, f32[96,256]{1,0:T(8,128)S(1)}, f32[96,256]{1,0:T(8,128)S(1)}, /*index=5*/f32[64,256]{1,0:T(8,128)S(1)}) custom-call(s32[65]{0:T(128)S(1)} %get-tuple-element.76.plan, f32[512,8]{1,0:T(8,128)S(1)} %get-tuple-element.75.prc, ...), custom_call_target="tpu_custom_call" | custom-call | tf_op jit(solution)/shard_map/pallas_call | solution.py:686
  51.3 4.1 %collective-permute-start.9 = (f32[96,256]{1,0:T(8,128)S(1)}, f32[96,256]{1,0:T(8,128)S(1)}, u32[]{:S(2)}, u32[]{:S(2)}) collective-permute-start(f32[96,256]{1,0:T(8,128)S(1)} %get-tuple-element.107), channel_id=1, source_target_pairs={{0,7},{1,0},{2,1},{3,2},{4,3},{5,4},{6,5},{7,6},{8,15},{9,8},{10,9... | collective-permute-start | bytes 294920 | tf_op jit(solution)/shard_map/ppermute | solution.py:613
  55.5 2.5 %shard_map.130 = (f32[512,128]{1,0:T(8,128)S(1)}, f32[8,128]{1,0:T(8,128)S(1)}) custom-call(s32[65]{0:T(128)S(1)} %get-tuple-element.76.plan, f32[512,8]{1,0:T(8,128)S(1)} %get-tuple-element.75.prc, f32[8,8,128]{2,1,0:T(8,128)S(1)} %get-tuple-element.81.xt, f32[512,128]{1,0:T(8,128)S(1)} %get-tuple-element.100.grad_acc, ...), custom_call_target="tpu_custom_call" | custom-call | tf_op jit(solution)/shard_map/pallas_call | solution.py:699
  58.2 0.6 collective-permute-start.11
  58.8 7.4 %shard_map.129 = (f32[512,256]{1,0:T(8,128)S(1)}, f32[1,512]{1,0:T(1,128)}) custom-call(s32[65]{0:T(128)S(1)} %get-tuple-element.82.plan, f32[512,8]{1,0:T(8,128)S(1)} %get-tuple-element.75.prc, f32[16,8,128]{2,1,0:T(8,128)S(1)} %get-tuple-element.74.xt, f32[512,128]{1,0:T(8,128)S(1)} %get-tuple-element.100.grad_acc, ...), custom_call_target="tpu_custom_call" | custom-call | tf_op jit(solution)/shard_map/pallas_call | solution.py:704
  66.2 2.8 %shard_map.131 = (f32[512,256]{1,0:T(8,128)S(1)}, f32[512,128]{1,0:T(8,128)S(1)}, f32[3,128]{1,0:T(4,128)S(1)}, f32[3,128]{1,0:T(4,128)S(1)}, f32[2,128]{1,0:T(2,128)S(1)}) custom-call(s32[65]{0:T(128)S(1)} %get-tuple-element.76.plan, f32[1,256]{1,0:T(1,128)S(1)} %get-tuple-element.62.lists, f32[512,8]{1,0:T(8,128)S(1)} %get-tuple-element.75.prc, ...), custom_call_target="tpu_custom_call" | custom-call | tf_op jit(solution)/shard_map/pallas_call | solution.py:707
  69.1 4.2 %collective-permute-start.13 = (f32[3,128]{1,0:T(4,128)S(1)}, f32[3,128]{1,0:T(4,128)S(1)}, u32[]{:S(2)}, u32[]{:S(2)}) collective-permute-start(f32[3,128]{1,0:T(4,128)S(1)} %get-tuple-element.118), channel_id=1, source_target_pairs={{0,7},{1,0},{2,1},{3,2},{4,3},{5,4},{6,5},{7,6},{8,15},{9,8},{10,9... | collective-permute-start | bytes 4616 | tf_op jit(solution)/shard_map/ppermute | solution.py:613
  73.3 1.5 %collective-permute-done.12.up = f32[3,128]{1,0:T(4,128)S(1)} collective-permute-done((f32[3,128]{1,0:T(4,128)S(1)}, f32[3,128]{1,0:T(4,128)S(1)}, u32[]{:S(2)}, u32[]{:S(2)}) %collective-permute-start.12) | collective-permute-done | bytes 1568 | tf_op jit(solution)/shard_map/ppermute | solution.py:612
  74.8 4.7 %collective-permute-start.14 = (f32[3,128]{1,0:T(4,128)S(1)}, f32[3,128]{1,0:T(4,128)S(1)}, u32[]{:S(2)}, u32[]{:S(2)}) collective-permute-start(f32[3,128]{1,0:T(4,128)S(1)} %pad_maximum_fusion.6), channel_id=1, source_target_pairs={{0,248},{8,0},{16,8},{24,16},{32,24},{40,32},{48,40},{56,48},{64,5... | collective-permute-start | bytes 4616 | tf_op jit(solution)/shard_map/ppermute | solution.py:616
  79.6 4.7 %shard_map.132.partial = f32[3,512]{1,0:T(4,128)S(1)} custom-call(s32[65]{0:T(128)S(1)} %get-tuple-element.82.plan, f32[512,8]{1,0:T(8,128)S(1)} %get-tuple-element.75.prc, f32[16,8,128]{2,1,0:T(8,128)S(1)} %get-tuple-element.74.xt, f32[512,256]{1,0:T(8,128)S(1)} %get-tuple-element.119.quad, f32[512,128]{1,0:T(8,128)S(1)} %get-tuple-element.100.grad_acc, ...), custom_call_target="tpu_custom_call" | custom-call | tf_op jit(solution)/shard_map/pallas_call | solution.py:715
  84.3 1.9 %collective-permute-done.15.right = f32[3,128]{1,0:T(4,128)S(1)} collective-permute-done((f32[3,128]{1,0:T(4,128)S(1)}, f32[3,128]{1,0:T(4,128)S(1)}, u32[]{:S(2)}, u32[]{:S(2)}) %collective-permute-start.15) | collective-permute-done | bytes 1568 | tf_op jit(solution)/shard_map/ppermute | solution.py:617
  86.2 0.9 %shard_map.133 = f32[3,512]{1,0:T(4,128)} custom-call(f32[1,256]{1,0:T(1,128)S(1)} %get-tuple-element.62.lists, f32[3,128]{1,0:T(4,128)S(1)} %collective-permute-done.14.left, f32[3,128]{1,0:T(4,128)S(1)} %collective-permute-done.15.right, f32[3,128]{1,0:T(4,128)S(1)} %collective-permute-done.12.up, f32[3,128]{1,0:T(4,128)S(1)} %collective-permute-done.13.down, ...), custom_call_target="tpu_custom_call" | custom-call | tf_op jit(solution)/shard_map/pallas_call | solution.py:721
  (53 shorter events, 1.3 us)
Async XLA Ops:
  0.6 0.7 copy-start.8
  1.3 0.7 copy-start.2
  2.0 0.7 copy-start.6
  2.7 4.7 %copy-start.5 = (f32[2,8,128]{2,1,0:T(8,128)S(1)}, f32[2,8,128]{2,1,0:T(8,128)}, u32[]{:S(2)}) copy-start(f32[2,8,128]{2,1,0:T(8,128)} %radial_two.1) | copy-start | bytes 24580
  2.7 4.7 %copy-start.7 = (f32[8,128]{1,0:T(8,128)S(1)}, f32[8,128]{1,0:T(8,128)}, u32[]{:S(2)}) copy-start(f32[8,128]{1,0:T(8,128)} %embed.1) | copy-start | bytes 12292
  3.1 4.2 %copy-start.4 = (f32[2,8,128]{2,1,0:T(8,128)S(1)}, f32[2,8,128]{2,1,0:T(8,128)}, u32[]{:S(2)}) copy-start(f32[2,8,128]{2,1,0:T(8,128)} %radial_one.1) | copy-start | bytes 24580
  3.1 7.0 %collective-permute-start = (f32[3,128]{1,0:T(4,128)S(1)}, f32[3,128]{1,0:T(4,128)S(1)}, u32[]{:S(2)}, u32[]{:S(2)}) collective-permute-start(f32[3,128]{1,0:T(4,128)S(1)} %get-tuple-element.63), channel_id=1, source_target_pairs={{0,1},{1,2},{2,3},{3,4},{4,5},{5,6},{6,7},{7,0},{8,9},{9,10},{10,1... | collective-permute-start | bytes 4616 | tf_op jit(solution)/shard_map/ppermute | solution.py:612
  4.8 5.4 %collective-permute-start.1 = (f32[3,128]{1,0:T(4,128)S(1)}, f32[3,128]{1,0:T(4,128)S(1)}, u32[]{:S(2)}, u32[]{:S(2)}) collective-permute-start(f32[3,128]{1,0:T(4,128)S(1)} %get-tuple-element.64), channel_id=1, source_target_pairs={{0,7},{1,0},{2,1},{3,2},{4,3},{5,4},{6,5},{7,6},{8,15},{9,8},{10,9... | collective-permute-start | bytes 4616 | tf_op jit(solution)/shard_map/ppermute | solution.py:613
  7.4 0.7 copy-start.9
  8.0 1.0 %copy-start = (f32[5,128,128]{2,1,0:T(8,128)S(1)}, f32[5,128,128]{2,1,0:T(8,128)}, u32[]{:S(2)}) copy-start(f32[5,128,128]{2,1,0:T(8,128)} %mix_one.1) | copy-start | bytes 983044
  9.0 0.9 %copy-start.1 = (f32[2,128,128]{2,1,0:T(8,128)S(1)}, f32[2,128,128]{2,1,0:T(8,128)}, u32[]{:S(2)}) copy-start(f32[2,128,128]{2,1,0:T(8,128)} %mix_two.1) | copy-start | bytes 393220
  10.2 11.1 %collective-permute-start.2 = (f32[3,128]{1,0:T(4,128)S(1)}, f32[3,128]{1,0:T(4,128)S(1)}, u32[]{:S(2)}, u32[]{:S(2)}) collective-permute-start(f32[3,128]{1,0:T(4,128)S(1)} %pad_maximum_fusion.4), channel_id=1, source_target_pairs={{0,248},{8,0},{16,8},{24,16},{32,24},{40,32},{48,40},{56,48},{64,5... | collective-permute-start | bytes 4616 | tf_op jit(solution)/shard_map/ppermute | solution.py:616
  15.9 6.7 %collective-permute-start.3 = (f32[3,128]{1,0:T(4,128)S(1)}, f32[3,128]{1,0:T(4,128)S(1)}, u32[]{:S(2)}, u32[]{:S(2)}) collective-permute-start(f32[3,128]{1,0:T(4,128)S(1)} %pad_maximum_fusion.5), channel_id=1, source_target_pairs={{0,8},{8,16},{16,24},{24,32},{32,40},{40,48},{48,56},{56,64},{64,7... | collective-permute-start | bytes 4616 | tf_op jit(solution)/shard_map/ppermute | solution.py:617
  16.6 0.7 copy-start.10
  17.3 5.3 %copy-start.3 = (s32[1,1,8,32]{3,2,1,0:T(8,128)S(1)}, s32[1,1,8,32]{3,2,1,0:T(8,128)}, u32[]{:S(2)}) copy-start(s32[1,1,8,32]{3,2,1,0:T(8,128)} %param.13) | copy-start | bytes 3076
  25.9 6.8 %collective-permute-start.4 = (f32[96,256]{1,0:T(8,128)S(1)}, f32[96,256]{1,0:T(8,128)S(1)}, u32[]{:S(2)}, u32[]{:S(2)}) collective-permute-start(f32[96,256]{1,0:T(8,128)S(1)} %get-tuple-element.83), channel_id=1, source_target_pairs={{0,1},{1,2},{2,3},{3,4},{4,5},{5,6},{6,7},{7,0},{8,9},{9,10},{10,1... | collective-permute-start | bytes 294920 | tf_op jit(solution)/shard_map/ppermute | solution.py:612
  26.0 6.7 %collective-permute-start.5 = (f32[96,256]{1,0:T(8,128)S(1)}, f32[96,256]{1,0:T(8,128)S(1)}, u32[]{:S(2)}, u32[]{:S(2)}) collective-permute-start(f32[96,256]{1,0:T(8,128)S(1)} %get-tuple-element.84), channel_id=1, source_target_pairs={{0,7},{1,0},{2,1},{3,2},{4,3},{5,4},{6,5},{7,6},{8,15},{9,8},{10,9... | collective-permute-start | bytes 294920 | tf_op jit(solution)/shard_map/ppermute | solution.py:613
  32.8 6.1 %collective-permute-start.6 = (f32[96,256]{1,0:T(8,128)S(1)}, f32[96,256]{1,0:T(8,128)S(1)}, u32[]{:S(2)}, u32[]{:S(2)}) collective-permute-start(f32[96,256]{1,0:T(8,128)S(1)} %pad_maximum_fusion), channel_id=1, source_target_pairs={{0,248},{8,0},{16,8},{24,16},{32,24},{40,32},{48,40},{56,48},{64,5... | collective-permute-start | bytes 294920 | tf_op jit(solution)/shard_map/ppermute | solution.py:616
  35.7 7.7 %collective-permute-start.7 = (f32[96,256]{1,0:T(8,128)S(1)}, f32[96,256]{1,0:T(8,128)S(1)}, u32[]{:S(2)}, u32[]{:S(2)}) collective-permute-start(f32[96,256]{1,0:T(8,128)S(1)} %pad_maximum_fusion.1), channel_id=1, source_target_pairs={{0,8},{8,16},{16,24},{24,32},{32,40},{40,48},{48,56},{56,64},{64,7... | collective-permute-start | bytes 294920 | tf_op jit(solution)/shard_map/ppermute | solution.py:617
  51.1 7.0 %collective-permute-start.8 = (f32[96,256]{1,0:T(8,128)S(1)}, f32[96,256]{1,0:T(8,128)S(1)}, u32[]{:S(2)}, u32[]{:S(2)}) collective-permute-start(f32[96,256]{1,0:T(8,128)S(1)} %get-tuple-element.106), channel_id=1, source_target_pairs={{0,1},{1,2},{2,3},{3,4},{4,5},{5,6},{6,7},{7,0},{8,9},{9,10},{10,1... | collective-permute-start | bytes 294920 | tf_op jit(solution)/shard_map/ppermute | solution.py:612
  51.3 6.7 %collective-permute-start.9 = (f32[96,256]{1,0:T(8,128)S(1)}, f32[96,256]{1,0:T(8,128)S(1)}, u32[]{:S(2)}, u32[]{:S(2)}) collective-permute-start(f32[96,256]{1,0:T(8,128)S(1)} %get-tuple-element.107), channel_id=1, source_target_pairs={{0,7},{1,0},{2,1},{3,2},{4,3},{5,4},{6,5},{7,6},{8,15},{9,8},{10,9... | collective-permute-start | bytes 294920 | tf_op jit(solution)/shard_map/ppermute | solution.py:613
  58.1 8.1 %collective-permute-start.10 = (f32[96,256]{1,0:T(8,128)S(1)}, f32[96,256]{1,0:T(8,128)S(1)}, u32[]{:S(2)}, u32[]{:S(2)}) collective-permute-start(f32[96,256]{1,0:T(8,128)S(1)} %pad_maximum_fusion.2), channel_id=1, source_target_pairs={{0,248},{8,0},{16,8},{24,16},{32,24},{40,32},{48,40},{56,48},{64,5... | collective-permute-start | bytes 294920 | tf_op jit(solution)/shard_map/ppermute | solution.py:616
  58.2 8.0 %collective-permute-start.11 = (f32[96,256]{1,0:T(8,128)S(1)}, f32[96,256]{1,0:T(8,128)S(1)}, u32[]{:S(2)}, u32[]{:S(2)}) collective-permute-start(f32[96,256]{1,0:T(8,128)S(1)} %pad_maximum_fusion.3), channel_id=1, source_target_pairs={{0,8},{8,16},{16,24},{24,32},{32,40},{40,48},{48,56},{56,64},{64,7... | collective-permute-start | bytes 294920 | tf_op jit(solution)/shard_map/ppermute | solution.py:617
  69.0 5.8 %collective-permute-start.12 = (f32[3,128]{1,0:T(4,128)S(1)}, f32[3,128]{1,0:T(4,128)S(1)}, u32[]{:S(2)}, u32[]{:S(2)}) collective-permute-start(f32[3,128]{1,0:T(4,128)S(1)} %get-tuple-element.116), channel_id=1, source_target_pairs={{0,1},{1,2},{2,3},{3,4},{4,5},{5,6},{6,7},{7,0},{8,9},{9,10},{10,1... | collective-permute-start | bytes 4616 | tf_op jit(solution)/shard_map/ppermute | solution.py:612
  69.1 5.7 %collective-permute-start.13 = (f32[3,128]{1,0:T(4,128)S(1)}, f32[3,128]{1,0:T(4,128)S(1)}, u32[]{:S(2)}, u32[]{:S(2)}) collective-permute-start(f32[3,128]{1,0:T(4,128)S(1)} %get-tuple-element.118), channel_id=1, source_target_pairs={{0,7},{1,0},{2,1},{3,2},{4,3},{5,4},{6,5},{7,6},{8,15},{9,8},{10,9... | collective-permute-start | bytes 4616 | tf_op jit(solution)/shard_map/ppermute | solution.py:613
  74.8 9.5 %collective-permute-start.14 = (f32[3,128]{1,0:T(4,128)S(1)}, f32[3,128]{1,0:T(4,128)S(1)}, u32[]{:S(2)}, u32[]{:S(2)}) collective-permute-start(f32[3,128]{1,0:T(4,128)S(1)} %pad_maximum_fusion.6), channel_id=1, source_target_pairs={{0,248},{8,0},{16,8},{24,16},{32,24},{40,32},{48,40},{56,48},{64,5... | collective-permute-start | bytes 4616 | tf_op jit(solution)/shard_map/ppermute | solution.py:616
  79.5 6.7 %collective-permute-start.15 = (f32[3,128]{1,0:T(4,128)S(1)}, f32[3,128]{1,0:T(4,128)S(1)}, u32[]{:S(2)}, u32[]{:S(2)}) collective-permute-start(f32[3,128]{1,0:T(4,128)S(1)} %pad_maximum_fusion.7), channel_id=1, source_target_pairs={{0,8},{8,16},{16,24},{24,32},{32,40},{40,48},{48,56},{56,64},{64,7... | collective-permute-start | bytes 4616 | tf_op jit(solution)/shard_map/ppermute | solution.py:617

commit v3 on v2

--- a/solution.py
+++ b/solution.py
@@ -20,6 +20,7 @@
 BF16 = jnp.bfloat16
 VMEM = pltpu.VMEM
 SMEM = pltpu.SMEM
+HBM = pltpu.HBM
 PARAMS = pltpu.CompilerParams(vmem_limit_bytes=32 * 1024 * 1024)
 CHUNK = 128
 HIST = 256
@@ -70,13 +71,6 @@
     low = jnp.concatenate([bl, jnp.zeros_like(bl)], axis=axis)
     out = mm(jnp.concatenate([ah, al], axis=1), jnp.concatenate([top, low], axis=1 - axis), dims)
     return out[:, :128] + out[:, 128:]
-
-
-def mm3_turned(a, b):
-    (ah, al), (bh, bl) = a, b
-    out = mm(jnp.concatenate([ah, al], axis=1), bh, TN)
-    width = ah.shape[1]
-    return out[:width] + (out[width:] + mm(ah, bl, TN))
 
 
 def iota(shape, dim):
@@ -191,10 +185,14 @@
     return split(jnp.concatenate(both, axis=0))
 
 
-def add_forward(r, c, keep, prc, xt, table, radial, acc):
+def pair_tile(r, c, keep, prc, xt):
     env, slope, scaled, vk = geometry(r, c, keep, prc, xt)
-    tile = split(jnp.concatenate(pair_parts(env, scaled, vk), axis=0))
-    prod = mm3_deep(tile, cell_features(table, c), NN)
+    return jnp.concatenate(split(jnp.concatenate(pair_parts(env, scaled, vk), axis=0)), axis=1)
+
+
+def add_forward(r, c, tile, table, radial, acc):
+    fh, fl = cell_features(table, c)
+    prod = mm(tile, jnp.concatenate([fh, fh], axis=0), NN) + mm(tile[:, :LANES], fl, NN)
     part = None
     for n in range(NB):
         rows = prod[n * CELL : (n + 1) * CELL]
@@ -203,10 +201,10 @@
     acc[cell_rows(r), :] += part
 
 
-def add_feature_grad(r, c, keep, prc, xt, grad_acc, radial, grad_table):
-    env, slope, scaled, vk = geometry(r, c, keep, prc, xt)
-    tile = split(jnp.concatenate(pair_parts(env, scaled, vk), axis=0))
-    gf = mm3_turned(tile, spread(grad_acc[cell_rows(r), :], radial))
+def add_feature_grad(r, c, tile, grad_acc, radial, grad_table):
+    uh, ul = spread(grad_acc[cell_rows(r), :], radial)
+    gf = mm(tile, uh, TN)
+    gf = gf[:LANES] + (gf[LANES:] + mm(tile[:, :LANES], ul, TN))
     grad_table[cell_rows(c), :] += jnp.concatenate(
         [gf[0:CELL, :CH]] + [gf[(t + 1) * CELL : (t + 2) * CELL, CH:] for t in range(3)], axis=1
     )
@@ -223,7 +221,7 @@
     def step(i, carry):
         for k in range(unroll):
             slot = i * unroll + k
-            body(plan[2 * slot], plan[2 * slot + 1], jnp.where(slot < count, 1.0, 0.0).astype(F32))
+            body(plan[2 * slot], plan[2 * slot + 1], jnp.where(slot < count, 1.0, 0.0).astype(F32), slot)
         return carry
 
     lax.fori_loop(0, (count + unroll - 1) // unroll, step, 0)
@@ -257,15 +255,20 @@
     return [at(right, 0), at(right, 1), at(right, 2), at(up, 1), at(down, 1), at(left, 0), at(left, 1), at(left, 2)]
 
 
-def pack_kernel(pos_in, species_in, lists_in, up, down, mid, table_out, row_out, pos, species, lists, sems):
-    copies = [
-        pltpu.make_async_copy(src, dst, sems.at[k])
-        for k, (src, dst) in enumerate(((pos_in, pos), (species_in, species), (lists_in, lists)))
-    ]
+def fetch(sems, *pairs):
+    copies = [pltpu.make_async_copy(src, dst, sems.at[k]) for k, (src, dst) in enumerate(pairs)]
     for copy in copies:
         copy.start()
+    return copies
+
+
+def arrive(copies):
     for copy in copies:
         copy.wait()
+
+
+def pack_kernel(pos_in, species_in, lists_in, up, down, mid, table_out, row_out, pos, species, lists, sems):
+    arrive(fetch(sems, (pos_in, pos), (species_in, species), (lists_in, lists)))
     kinds = species[...].astype(F32)
     table = jnp.concatenate([kinds, pos[...], jnp.zeros((4, kinds.shape[1]), F32)], axis=0)
     table_out[...] = table
@@ -284,9 +287,49 @@
 
 
 def weight_kernel(
-    table, embed, radial_one, mix_one, radial_two, mix_two, readout,
-    w_hi, w_lo, mats, begins, radial, rows, xt, prc,
+    count, table, row, pairs_in, lists_in, embed_in, radial_one_in, mix_one_in, radial_two_in, mix_two_in, readout_in,
+    w_hi, w_lo, mats, begins, radial, rows, xt, prc, hot, plan_own, plan_ghost, lists_out,
+    pairs, embed, radial_one, mix_one, radial_two, mix_two, readout, sems,
 ):
+    sources = (pairs_in, lists_in, embed_in, radial_one_in, mix_one_in, radial_two_in, mix_two_in, readout_in)
+    targets = (pairs, lists_out, embed, radial_one, mix_one, radial_two, mix_two, readout)
+    copies = fetch(sems, *zip(sources, targets))
+    lists = row[...].astype(jnp.int32)
+    hot[...] = jnp.where(iota(hot.shape, 0) == lists, 1.0, 0.0).astype(BF16)
+    t = table[...]
+    for c in range(OWN):
+        xt[c] = tile_group(t[:, (c // 4) * LANES : (c // 4 + 1) * LANES], c % 4)
+    prc[...] = jnp.concatenate([t[1:4], t[0:1], t[4:8]], axis=0).T
+    arrive(copies[:1])
+    def clear(i, carry):
+        plan_own[i] = 0
+        plan_ghost[i] = 0
+        return carry
+
+    lax.fori_loop(0, 2 * SLOTS, clear, 0)
+
+    def sort(i, carry):
+        n_own, n_ghost = carry
+        r, c = pairs[0, i], pairs[1, i]
+        mine = c < OWN
+
+        @pl.when(mine)
+        def _():
+            plan_own[2 * n_own] = r
+            plan_own[2 * n_own + 1] = c
+
+        @pl.when(jnp.logical_not(mine))
+        def _():
+            plan_ghost[2 * n_ghost] = r
+            plan_ghost[2 * n_ghost + 1] = c - OWN
+
+        step = mine.astype(jnp.int32)
+        return n_own + step, n_ghost + 1 - step
+
+    n_own, n_ghost = lax.fori_loop(0, count[0, 0], sort, (jnp.int32(0), jnp.int32(0)))
+    plan_own[2 * SLOTS] = n_own
+    plan_ghost[2 * SLOTS] = n_ghost
+    arrive(copies[1:])
     w_hi[...], w_lo[...] = species_weights(embed[...], 0.5 * radial_one[...])
     for k, m in enumerate((mix_one[0], mix_one[4], mix_one[1], mix_one[3], mix_two[0])):
         mats[0, k * CH : (k + 1) * CH, :], mats[1, k * CH : (k + 1) * CH, :] = split(m)
@@ -295,44 +338,12 @@
     both = readout[...]
     rows[0:1, :] = both[0:1, :] + mm3(split(both), split(mix_two[1]), NN)[1:2, :]
     rows[1:2, :] = both[1:2, :]
-    t = table[...]
-    for c in range(OWN):
-        xt[c] = tile_group(t[:, (c // 4) * LANES : (c // 4 + 1) * LANES], c % 4)
-    prc[...] = jnp.concatenate([t[1:4], t[0:1], t[4:8]], axis=0).T
-
-
-def own_first_kernel(pairs, count, xt, prc, plan_own, plan_ghost, hist):
-    def clear(i, carry):
-        plan_own[i] = 0
-        plan_ghost[i] = 0
-        return carry
-
-    lax.fori_loop(0, 2 * SLOTS, clear, 0)
-
-    def sort(i, carry):
-        n_own, n_ghost = carry
-        r, c = pairs[0, i], pairs[1, i]
-        mine = c < OWN
-
-        @pl.when(mine)
-        def _():
-            plan_own[2 * n_own] = r
-            plan_own[2 * n_own + 1] = c
-
-        @pl.when(jnp.logical_not(mine))
-        def _():
-            plan_ghost[2 * n_ghost] = r
-            plan_ghost[2 * n_ghost + 1] = c - OWN
-
-        step = mine.astype(jnp.int32)
-        return n_own + step, n_ghost + 1 - step
-
-    n_own, n_ghost = lax.fori_loop(0, count[0, 0], sort, (jnp.int32(0), jnp.int32(0)))
-    plan_own[2 * SLOTS] = n_own
-    plan_ghost[2 * SLOTS] = n_ghost
+
+
+def own_first_kernel(plan_own, xt, prc, hist):
     hist[...] = jnp.zeros_like(hist)
 
-    def block(r, c, weight):
+    def block(r, c, weight, slot):
         add_histogram(r, c, own_keep(r, c, weight), prc, xt, hist)
 
     for_blocks(plan_own, UNROLL_OWN, block)
@@ -349,7 +360,7 @@
             xt[p, k : k + 1, :] = part[p : p + 1, :] + shift
     hist[...] = hist_own[...]
 
-    def block(r, c, weight):
+    def block(r, c, weight, slot):
         add_histogram(r, c, weight, prc, xt, hist)
 
     for_blocks(plan, UNROLL_GHOST, block)
@@ -428,17 +439,24 @@
     lax.fori_loop(0, feat.shape[0] // CHUNK, chunk, 0)
 
 
-def own_second_kernel(plan, prc, xt, feat, radial, acc):
+def own_second_kernel(plan, plan_ghost, prc, xt, xt_ghost, feat, radial, acc, tiles, tiles_ghost):
     acc[...] = jnp.zeros_like(acc)
 
-    def block(r, c, weight):
-        add_forward(r, c, own_keep(r, c, weight), prc, xt, feat, radial, acc)
+    def block(r, c, weight, slot):
+        tile = pair_tile(r, c, own_keep(r, c, weight), prc, xt)
+        tiles[slot] = tile
+        add_forward(r, c, tile, feat, radial, acc)
 
     for_blocks(plan, UNROLL_OWN, block)
 
+    def ghost(r, c, weight, slot):
+        tiles_ghost[slot] = pair_tile(r, c, weight, prc, xt_ghost)
+
+    for_blocks(plan_ghost, UNROLL_GHOST, ghost)
+
 
 def ghost_second_kernel(
-    plan, prc, xt, left, right, up, down, w_hi, w_lo, begins, mats, acc_own, radial, readout,
+    plan, tiles, xt, left, right, up, down, w_hi, w_lo, begins, mats, acc_own, radial, readout,
     acc, grad_acc, feat, send_up, send_down, send_mid,
     joined, lin, gates, lifted, grad_table,
 ):
@@ -456,8 +474,8 @@
         out = first_update(joined[rows, :], kind, (w_hi[...], w_lo[...]), begin, *mix_all)
         feat[rows, :], lin[rows, :], gates[rows, :], lifted[rows, :] = out
 
-    def forward(r, c, weight):
-        add_forward(r, c, weight, prc, xt, feat, radial, acc)
+    def forward(r, c, weight, slot):
+        add_forward(r, c, tiles[slot], feat, radial, acc)
 
     for_blocks(plan, UNROLL_GHOST, forward)
 
@@ -473,8 +491,8 @@
 
     lax.fori_loop(0, acc.shape[0] // CHUNK, chunk, 0)
 
-    def backward(r, c, weight):
-        add_feature_grad(r, c, weight, prc, xt, grad_acc, radial, grad_table)
+    def backward(r, c, weight, slot):
+        add_feature_grad(r, c, tiles[slot], grad_acc, radial, grad_table)
 
     for_blocks(plan, UNROLL_GHOST, backward)
 
@@ -488,29 +506,19 @@
 
 
 def own_grad_kernel(
-    plan, prc, xt, grad_acc, radial, acc, feat, lin, gates, lifted, w_hi, w_lo, mats, readout,
-    quad, energy,
+    plan, tiles, grad_acc, radial, lin, gates, lifted, w_hi, w_lo, mats, readout,
+    quad,
     grad_table,
 ):
-    atoms = feat.shape[0]
+    atoms = quad.shape[0]
     grad_table[...] = jnp.zeros_like(grad_table)
 
-    def block(r, c, weight):
-        add_feature_grad(r, c, own_keep(r, c, weight), prc, xt, grad_acc, radial, grad_table)
+    def block(r, c, weight, slot):
+        add_feature_grad(r, c, tiles[slot], grad_acc, radial, grad_table)
 
     for_blocks(plan, UNROLL_OWN, block)
     mix_all = mixes(mats)
-    mix0 = mat(mats, 4 * CH, CH)
     carry_w = readout[0:1, :]
-    row8 = iota((8, CH), 0)
-    first = split(jnp.where(row8 == 0, carry_w, 0.0))
-    second = split(jnp.where(row8 == 0, readout[1:2, :], 0.0))
-    for i in range(atoms // CHUNK):
-        rows = pl.ds(i * CHUNK, CHUNK)
-        z = mm3_full(split(acc[rows, :]), mix0, NT)
-        s1 = feat[rows, :][:, :CH]
-        e = mm3(first, split(s1), NT) + mm3(second, split(z * jax.nn.sigmoid(z)), NT)
-        energy[:, i * CHUNK : (i + 1) * CHUNK] = e[0:1, :]
 
     def chunk(i, carry):
         rows = chunk_rows(i)
@@ -527,7 +535,7 @@
     recv[...] = jnp.zeros_like(recv)
     send[...] = jnp.zeros_like(send)
 
-    def block(r, c, weight):
+    def block(r, c, weight, slot):
         env, slope, scaled, vk = geometry(r, c, weight, prc, xt)
         deriv = second_deriv(r, c, grad_acc, radial, feat)
         add_force(pair_force(deriv, env, slope, scaled, vk), r, c, recv, send)
@@ -536,7 +544,7 @@
 
 
 def ghost_last_kernel(
-    plan, lists, prc, xt, quad_own, left, right, up, down, recv_two, send_two,
+    plan, hot, prc, xt, quad_own, left, right, up, down, recv_two, send_two,
     quad, recv, send_up, send_down, send_mid,
     back_hi, back_lo, send,
 ):
@@ -546,17 +554,16 @@
         back_lo[p * CELL : (p + 1) * CELL, :] = lo
     recv[...] = recv_two[...]
     send[...] = send_two[...]
-    row = lists[...].astype(jnp.int32)
 
     def chunk(i, carry):
         rows = chunk_rows(i)
-        hot = jnp.where(iota((CHUNK, row.shape[1]), 0) + i * CHUNK == row, 1.0, 0.0).astype(BF16)
-        quad[rows, :] = quad_own[rows, :] + (mm(hot, back_hi[...], NN) + mm(hot, back_lo[...], NN))
+        pick = hot[rows, :]
+        quad[rows, :] = quad_own[rows, :] + (mm(pick, back_hi[...], NN) + mm(pick, back_lo[...], NN))
         return carry
 
     lax.fori_loop(0, quad.shape[0] // CHUNK, chunk, 0)
 
-    def block(r, c, weight):
+    def block(r, c, weight, slot):
         env, slope, scaled, vk = geometry(r, c, weight, prc, xt)
         add_force(pair_force(first_deriv(r, c, xt, quad), env, slope, scaled, vk), r, c, recv, send)
 
@@ -572,11 +579,13 @@
     return lines
 
 
-def own_force_kernel(plan, prc, xt, quad, grad_acc, radial, feat, recv_ghost, out, recv, send):
+def own_force_kernel(
+    plan, prc, xt, quad, grad_acc, radial, feat, recv_ghost, acc, mats, readout, out, energy, recv, send
+):
     recv[...] = recv_ghost[...]
     send[...] = jnp.zeros_like(send)
 
-    def block(r, c, weight):
+    def block(r, c, weight, slot):
         env, slope, scaled, vk = geometry(r, c, own_keep(r, c, weight), prc, xt)
         one = first_deriv(r, c, xt, quad)
         two = second_deriv(r, c, grad_acc, radial, feat)
@@ -588,16 +597,25 @@
     hi, lo = split(recv[...])
     total = mm(pick, hi, NT) + mm(pick, lo, NT)
     out[...] = total[0:3, :] - jnp.concatenate(by_axis(send, OWN), axis=0)
-
-
-def last_kernel(lists, left, right, up, down, partial, out):
+    mix0 = mat(mats, 4 * CH, CH)
+    carry_w = readout[0:1, :]
+    row8 = iota((8, CH), 0)
+    first = split(jnp.where(row8 == 0, carry_w, 0.0))
+    second = split(jnp.where(row8 == 0, readout[1:2, :], 0.0))
+    for i in range(feat.shape[0] // CHUNK):
+        rows = pl.ds(i * CHUNK, CHUNK)
+        z = mm3_full(split(acc[rows, :]), mix0, NT)
+        s1 = feat[rows, :][:, :CH]
+        e = mm3(first, split(s1), NT) + mm3(second, split(z * jax.nn.sigmoid(z)), NT)
+        energy[:, i * CHUNK : (i + 1) * CHUNK] = e[0:1, :]
+
+
+def last_kernel(hot, left, right, up, down, partial, out):
     rows = jnp.concatenate(arrived(left, right, up, down, 1), axis=0)
     lines = by_axis(rows, 8)
     back = jnp.concatenate(lines + [jnp.zeros((5, lines[0].shape[1]), F32)], axis=0)
     hi, lo = split(back)
-    row = lists[...].astype(jnp.int32)
-    hot = jnp.where(iota((partial.shape[1], row.shape[1]), 0) == row, 1.0, 0.0).astype(BF16)
-    ghost = mm(hi, hot, NT) + mm(lo, hot, NT)
+    ghost = mm(hi, hot[...], NT) + mm(lo, hot[...], NT)
     out[...] = partial[...] - ghost[0:3, :]
 
 
@@ -616,6 +634,10 @@
     left = lax.ppermute(jnp.concatenate([part(up, 0), part(mid, 0), part(down, 0)]), "gx", ring("gx", -1))
     right = lax.ppermute(jnp.concatenate([part(up, 2), part(mid, 1), part(down, 2)]), "gx", ring("gx", 1))
     return (left, right, up, down), between
+
+
+def in_hbm(*arrays):
+    return [pltpu.with_memory_space_constraint(x, HBM) for x in arrays]
 
 
 def call(kernel, outs, specs, scratch=()):
@@ -648,41 +670,45 @@
     *sends, table, row = call(
         pack_kernel,
         three(1, LANES) + [f(8, atoms), f(1, ghosts)],
-        [pl.ANY] * 3,
+        [HBM] * 3,
         [
             VMEM((3, atoms), F32),
             VMEM((1, atoms), jnp.int32),
             VMEM((8, CELL), jnp.int32),
             pltpu.SemaphoreType.DMA((3,)),
         ],
-    )(positions, kinds, lists)
+    )(*in_hbm(positions, kinds, lists))
     ready = call(
         weight_kernel,
         [
             b(HIST, FEAT), b(HIST, FEAT), b(2, 5 * CH, CH), b(2, NB, CH), f(2, NB, CH), f(2, CH),
-            f(OWN, 8, LANES), f(atoms, 8),
+            f(OWN, 8, LANES), f(atoms, 8), b(atoms, ghosts),
+            i(2 * SLOTS + 1), i(2 * SLOTS + 1), i(8, CELL),
         ],
-        [VMEM] * 7,
-    )(table, embed, radial_one, mix_one, radial_two, mix_two, readout)
+        [SMEM] + [VMEM] * 2 + [HBM] * 8,
+        [SMEM(pairs.shape, jnp.int32)]
+        + [VMEM(x.shape, F32) for x in (embed, radial_one, mix_one, radial_two, mix_two, readout)]
+        + [pltpu.SemaphoreType.DMA((8,))],
+    )(block_count, table, row, *in_hbm(pairs, lists, embed, radial_one, mix_one, radial_two, mix_two, readout))
     moved, ready = exchange(*sends, ready)
-    w_hi, w_lo, mats, begins, radial, rows, xt_own, prc = ready
-    plan_own, plan_ghost, hist_own = call(
-        own_first_kernel, [i(2 * SLOTS + 1), i(2 * SLOTS + 1), f(atoms, HIST)], [SMEM] * 2 + [VMEM] * 2
-    )(pairs, block_count, xt_own, prc)
+    w_hi, w_lo, mats, begins, radial, rows, xt_own, prc, hot, plan_own, plan_ghost, lists_s = ready
+    (hist_own,) = call(own_first_kernel, [f(atoms, HIST)], [SMEM] + [VMEM] * 2)(plan_own, xt_own, prc)
     hist, xt_ghost, *sends = call(
         functools.partial(ghost_first_kernel, side),
         [f(atoms, HIST), f(8, 8, LANES)] + three(CELL, HIST),
         [SMEM] * 2 + [VMEM] * 6,
-    )(plan_ghost, lists, *moved, prc, hist_own)
+    )(plan_ghost, lists_s, *moved, prc, hist_own)
 
     own = call(
         own_update_kernel, [f(atoms, FEAT), f(atoms, FEAT), f(atoms, 2 * CH), f(atoms, 3 * CH)], [VMEM] * 6
     )(hist, prc, w_hi, w_lo, begins, mats)
     moved, own = exchange(*sends, own)
     feat, lin, gates, lifted = own
-    (acc_own,) = call(own_second_kernel, [f(atoms, CH)], [SMEM] + [VMEM] * 4)(
-        plan_own, prc, xt_own, feat, radial
-    )
+    acc_own, tiles_own, tiles_ghost = call(
+        own_second_kernel,
+        [f(atoms, CH), b(SLOTS, HIST, 2 * LANES), b(SLOTS // 2, HIST, 2 * LANES)],
+        [SMEM] * 2 + [VMEM] * 5,
+    )(plan_own, plan_ghost, prc, xt_own, xt_ghost, feat, radial)
     acc, grad_acc, feat_ghost, *sends = call(
         ghost_second_kernel,
         [f(atoms, CH), f(atoms, CH), f(ghosts, FEAT)] + three(CELL, HIST),
@@ -694,31 +720,31 @@
             VMEM((ghosts, 3 * CH), F32),
             VMEM((ghosts, FEAT), F32),
         ],
-    )(plan_ghost, prc, xt_ghost, *moved, w_hi, w_lo, begins, mats, acc_own, radial, rows)
+    )(plan_ghost, tiles_ghost, xt_ghost, *moved, w_hi, w_lo, begins, mats, acc_own, radial, rows)
 
     two = call(ghost_force_kernel, [f(atoms, LANES), f(8, LANES)], [SMEM] + [VMEM] * 5)(
         plan_ghost, prc, xt_ghost, grad_acc, radial, feat_ghost
     )
     moved, two = exchange(*sends, two)
     recv_two, send_two = two
-    quad_own, energy = call(
-        own_grad_kernel, [f(atoms, HIST), f(1, atoms)], [SMEM] + [VMEM] * 13, [VMEM((atoms, FEAT), F32)]
-    )(plan_own, prc, xt_own, grad_acc, radial, acc, feat, lin, gates, lifted, w_hi, w_lo, mats, rows)
+    (quad_own,) = call(
+        own_grad_kernel, [f(atoms, HIST)], [SMEM] + [VMEM] * 10, [VMEM((atoms, FEAT), F32)]
+    )(plan_own, tiles_own, grad_acc, radial, lin, gates, lifted, w_hi, w_lo, mats, rows)
     quad, recv, *sends = call(
         ghost_last_kernel,
         [f(atoms, HIST), f(atoms, LANES)] + three(1, LANES),
         [SMEM] + [VMEM] * 10,
         [VMEM((ghosts, HIST), BF16), VMEM((ghosts, HIST), BF16), VMEM((8, LANES), F32)],
-    )(plan_ghost, row, prc, xt_ghost, quad_own, *moved, recv_two, send_two)
+    )(plan_ghost, hot, prc, xt_ghost, quad_own, *moved, recv_two, send_two)
 
     moved, unused = exchange(*sends)
-    (partial,) = call(
+    partial, energy = call(
         own_force_kernel,
-        [f(3, atoms)],
-        [SMEM] + [VMEM] * 7,
+        [f(3, atoms), f(1, atoms)],
+        [SMEM] + [VMEM] * 10,
         [VMEM((atoms, LANES), F32), VMEM((OWN, LANES), F32)],
-    )(plan_own, prc, xt_own, quad, grad_acc, radial, feat, recv)
-    (forces,) = call(last_kernel, [f(3, atoms)], [VMEM] * 6)(row, *moved, partial)
+    )(plan_own, prc, xt_own, quad, grad_acc, radial, feat, recv, acc, mats, rows)
+    (forces,) = call(last_kernel, [f(3, atoms)], [VMEM] * 6)(hot, *moved, partial)
     return forces, energy[0]
 
 

time: 88.5 us -> 82.1 us (0.928)
  the two profiles are of different devices: /device:TPU:6 before, /device:TPU:24 now
where the time goes in v3:
time: 82.1 us; the launch traced here: 81.2 us
  Pallas kernels  39.5 us (48%)
  waiting for transfers between devices  22.2 us (27%)
  starting transfers between devices  17.9 us (22%)
  between operations  1.47 us (2%)
    ppermute x4, waiting for transfers between devices, exchange(): lax.ppermute(jnp.concatenate([part(up, 2), part(mid, 1), part(down, 2)]),...  10.3 us
    ppermute x4, waiting for transfers between devices, exchange(): down = lax.ppermute(down, 'gy', ring('gy', -1))  10 us
    ppermute x4, starting transfers between devices, exchange(): lax.ppermute(jnp.concatenate([part(up, 0), part(mid, 0), part(down, 0)]),...  8.55 us
    pallas_call x1, Pallas kernels, shards(): call(ghost_second_kernel, [f(atoms, CH), f(atoms, CH), f(ghosts, FEAT)] +...  6.54 us
    pallas_call x1, Pallas kernels, shards(): call(own_force_kernel, [f(3, atoms), f(1, atoms)], [SMEM] + [VMEM] * 10,...  5.96 us
    ppermute x4, starting transfers between devices, exchange(): down = lax.ppermute(down, 'gy', ring('gy', -1))  5.23 us
    pallas_call x1, Pallas kernels, shards(): call(own_grad_kernel, [f(atoms, HIST)], [SMEM] + [VMEM] * 10, [VMEM((atom...  5.1 us
    pallas_call x1, Pallas kernels, shards(): call(own_second_kernel, [f(atoms, CH), b(SLOTS, HIST, 2 * LANES), b(SLOTS...  3.93 us
  transfers between devices with their start and end apart: 16, of which 11 were waited for; matrix products, arithmetic and copies ran while one was open for 0% of the time, Pallas kernels for 31%

profile of v3, /device:TPU:24, one launch (start us, length us, event | category | flops | bytes accessed | tf_op | source)
XLA Modules:
  0.0 81.2 jit_solution(17272357192110173599)
XLA Ops:
  0.6 1.1 %shard_map.122 = (f32[3,128]{1,0:T(4,128)S(1)}, f32[3,128]{1,0:T(4,128)S(1)}, f32[2,128]{1,0:T(2,128)S(1)}, f32[8,512]{1,0:T(8,128)S(1)}, f32[1,256]{1,0:T(1,128)S(1)}) custom-call(f32[3,512]{1,0:T(4,128)} %pos_in.1, s32[1,512]{1,0:T(1,128)} %bitcast.8, s32[8,32]{1,0:T(8,128)} %bitcast.6), custom_call_target="tpu_custom_call" | custom-call | tf_op jit(solution)/shard_map/pallas_call | solution.py:670
  1.8 1.2 %collective-permute-start = (f32[3,128]{1,0:T(4,128)S(1)}, f32[3,128]{1,0:T(4,128)S(1)}, u32[]{:S(2)}, u32[]{:S(2)}) collective-permute-start(f32[3,128]{1,0:T(4,128)S(1)} %get-tuple-element.70), channel_id=1, source_target_pairs={{0,1},{1,2},{2,3},{3,4},{4,5},{5,6},{6,7},{7,0},{8,9},{9,10},{10,1... | collective-permute-start | bytes 4616 | tf_op jit(solution)/shard_map/ppermute | solution.py:630
  3.0 0.9 %collective-permute-start.1 = (f32[3,128]{1,0:T(4,128)S(1)}, f32[3,128]{1,0:T(4,128)S(1)}, u32[]{:S(2)}, u32[]{:S(2)}) collective-permute-start(f32[3,128]{1,0:T(4,128)S(1)} %get-tuple-element.71), channel_id=1, source_target_pairs={{0,7},{1,0},{2,1},{3,2},{4,3},{5,4},{6,5},{7,6},{8,15},{9,8},{10,9... | collective-permute-start | bytes 4616 | tf_op jit(solution)/shard_map/ppermute | solution.py:631
  4.5 2.3 %shard_map.123 = (bf16[256,512]{1,0:T(8,128)(2,1)S(1)}, bf16[256,512]{1,0:T(8,128)(2,1)S(1)}, bf16[2,640,128]{2,1,0:T(8,128)(2,1)S(1)}, bf16[2,8,128]{2,1,0:T(8,...) custom-call(s32[1,1]{1,0:T(1,128)S(6)} %copy.13.count, ...), custom_call_target="tpu_custom_call" | custom-call | tf_op jit(solution)/shard_map/pallas_call | solution.py:681
  6.9 1.8 %collective-permute-done.1.down = f32[3,128]{1,0:T(4,128)S(1)} collective-permute-done((f32[3,128]{1,0:T(4,128)S(1)}, f32[3,128]{1,0:T(4,128)S(1)}, u32[]{:S(2)}, u32[]{:S(2)}) %collective-permute-start.1) | collective-permute-done | bytes 1568 | tf_op jit(solution)/shard_map/ppermute | solution.py:631
  8.7 6.1 %collective-permute-start.2 = (f32[3,128]{1,0:T(4,128)S(1)}, f32[3,128]{1,0:T(4,128)S(1)}, u32[]{:S(2)}, u32[]{:S(2)}) collective-permute-start(f32[3,128]{1,0:T(4,128)S(1)} %pad_maximum_fusion.4), channel_id=1, source_target_pairs={{0,248},{8,0},{16,8},{24,16},{32,24},{40,32},{48,40},{56,48},{64,5... | collective-permute-start | bytes 4616 | tf_op jit(solution)/shard_map/ppermute | solution.py:634
  14.9 2.7 %shard_map.124.hist_own = f32[512,256]{1,0:T(8,128)S(1)} custom-call(s32[65]{0:T(128)S(1)} %get-tuple-element.93.plan_own.plan, f32[16,8,128]{2,1,0:T(8,128)S(1)} %get-tuple-element.94.xt, f32[512,8]{1,0:T(8,128)S(1)} %get-tuple-element.88.prc), custom_call_target="tpu_custom_call" | custom-call | tf_op jit(solution)/shard_map/pallas_call | solution.py:695
  17.6 3.9 %collective-permute-done.3.right = f32[3,128]{1,0:T(4,128)S(1)} collective-permute-done((f32[3,128]{1,0:T(4,128)S(1)}, f32[3,128]{1,0:T(4,128)S(1)}, u32[]{:S(2)}, u32[]{:S(2)}) %collective-permute-start.3) | collective-permute-done | bytes 1568 | tf_op jit(solution)/shard_map/ppermute | solution.py:635
  21.5 3.3 %shard_map.125 = (f32[512,256]{1,0:T(8,128)S(1)}, f32[8,8,128]{2,1,0:T(8,128)S(1)}, f32[96,256]{1,0:T(8,128)S(1)}, f32[96,256]{1,0:T(8,128)S(1)}, f32[64,256]{1,0:T(8,128)S(1)}) custom-call(s32[65]{0:T(128)S(1)} %get-tuple-element.87.plan.plan_ghost, s32[8,32]{1,0:T(8,128)S(1)} %get-tuple-element.89.lists, f32[3,128]{1,0:T(4,128)S(1)} %collective-permute-done.2.left, ...), custom_call_target="tpu_custom_call" | custom-call | tf_op jit(solution)/shard_map/pallas_call | solution.py:696
  24.8 1.8 %collective-permute-start.4 = (f32[96,256]{1,0:T(8,128)S(1)}, f32[96,256]{1,0:T(8,128)S(1)}, u32[]{:S(2)}, u32[]{:S(2)}) collective-permute-start(f32[96,256]{1,0:T(8,128)S(1)} %get-tuple-element.96), channel_id=1, source_target_pairs={{0,1},{1,2},{2,3},{3,4},{4,5},{5,6},{6,7},{7,0},{8,9},{9,10},{10,1... | collective-permute-start | bytes 294920 | tf_op jit(solution)/shard_map/ppermute | solution.py:630
  26.6 0.3 collective-permute-start.5
  26.9 2.3 %shard_map.126 = (f32[512,512]{1,0:T(8,128)S(1)}, f32[512,512]{1,0:T(8,128)S(1)}, f32[512,256]{1,0:T(8,128)S(1)}, f32[512,384]{1,0:T(8,128)S(1)}) custom-call(f32[512,256]{1,0:T(8,128)S(1)} %get-tuple-element.98.joined, f32[512,8]{1,0:T(8,128)S(1)} %get-tuple-element.88.prc, bf16[256,512]{1,0:T(8,128)(2,1)S(1)} %get-tuple-element.99.w_hi, ...), custom_call_target="tpu_custom_call" | custom-call | tf_op jit(solution)/shard_map/pallas_call | solution.py:702
  29.5 3.8 %collective-permute-done.5.down = f32[96,256]{1,0:T(8,128)S(1)} collective-permute-done((f32[96,256]{1,0:T(8,128)S(1)}, f32[96,256]{1,0:T(8,128)S(1)}, u32[]{:S(2)}, u32[]{:S(2)}) %collective-permute-start.5) | collective-permute-done | bytes 98336 | tf_op jit(solution)/shard_map/ppermute | solution.py:631
  33.5 0.6 collective-permute-start.7
  34.0 3.9 %shard_map.127 = (f32[512,128]{1,0:T(8,128)S(1)}, bf16[32,256,256]{2,1,0:T(8,128)(2,1)S(1)}, bf16[16,256,256]{2,1,0:T(8,128)(2,1)S(1)}) custom-call(s32[65]{0:T(128)S(1)} %get-tuple-element.93.plan_own.plan, s32[65]{0:T(128)S(1)} %get-tuple-element.87.plan.plan_ghost, f32[512,8]{1,0:T(8,128)S(1)} %get-tuple-element.88.prc, ...), custom_call_target="tpu_custom_call" | custom-call | tf_op jit(solution)/shard_map/pallas_call | solution.py:707
  38.0 3.2 %collective-permute-done.7.right = f32[96,256]{1,0:T(8,128)S(1)} collective-permute-done((f32[96,256]{1,0:T(8,128)S(1)}, f32[96,256]{1,0:T(8,128)S(1)}, u32[]{:S(2)}, u32[]{:S(2)}) %collective-permute-start.7) | collective-permute-done | bytes 98336 | tf_op jit(solution)/shard_map/ppermute | solution.py:635
  41.2 6.5 %shard_map.128 = (f32[512,128]{1,0:T(8,128)S(1)}, f32[512,128]{1,0:T(8,128)S(1)}, f32[256,512]{1,0:T(8,128)S(1)}, f32[96,256]{1,0:T(8,128)S(1)}, f32[96,256]{1,0:T(8,128)S(1)}, /*index=5*/f32[64,256]{1,0:T(8,128)S(1)}) custom-call(s32[65]{0:T(128)S(1)} %get-tuple-element.87.plan.plan_ghost, bf16[16,256,256]{2,1,0:T(8,128)(2,1)S(1)} %get-tuple-element.110.tiles, ...), custom_call_target="tpu_custom_call" | custom-call | tf_op jit(solution)/shard_map/pallas_call | solution.py:712
  47.7 0.3 collective-permute-start.8
  48.0 2.0 %collective-permute-start.9 = (f32[96,256]{1,0:T(8,128)S(1)}, f32[96,256]{1,0:T(8,128)S(1)}, u32[]{:S(2)}, u32[]{:S(2)}) collective-permute-start(f32[96,256]{1,0:T(8,128)S(1)} %get-tuple-element.121), channel_id=1, source_target_pairs={{0,7},{1,0},{2,1},{3,2},{4,3},{5,4},{6,5},{7,6},{8,15},{9,8},{10,9... | collective-permute-start | bytes 294920 | tf_op jit(solution)/shard_map/ppermute | solution.py:631
  50.0 2.5 %shard_map.130 = (f32[512,128]{1,0:T(8,128)S(1)}, f32[8,128]{1,0:T(8,128)S(1)}) custom-call(s32[65]{0:T(128)S(1)} %get-tuple-element.87.plan.plan_ghost, f32[512,8]{1,0:T(8,128)S(1)} %get-tuple-element.88.prc, f32[8,8,128]{2,1,0:T(8,128)S(1)} %get-tuple-element.95.xt_ghost.xt, f32[512,128]{1,0:T(8,128)S(1)} %get-tuple-element.116.grad_acc, ...), custom_call_target="tpu_custom_call" | custom-call | tf_op jit(solution)/shard_map/pallas_call | solution.py:725
  52.6 2.2 %collective-permute-done.9.down = f32[96,256]{1,0:T(8,128)S(1)} collective-permute-done((f32[96,256]{1,0:T(8,128)S(1)}, f32[96,256]{1,0:T(8,128)S(1)}, u32[]{:S(2)}, u32[]{:S(2)}) %collective-permute-start.9) | collective-permute-done | bytes 98336 | tf_op jit(solution)/shard_map/ppermute | solution.py:631
  54.8 0.6 collective-permute-start.10
  55.5 5.1 %shard_map.129.quad_own = f32[512,256]{1,0:T(8,128)S(1)} custom-call(s32[65]{0:T(128)S(1)} %get-tuple-element.93.plan_own.plan, bf16[32,256,256]{2,1,0:T(8,128)(2,1)S(1)} %get-tuple-element.109.tiles, f32[512,128]{1,0:T(8,128)S(1)} %get-tuple-element.116.grad_acc, f32[2,8,128]{2,1,0:T(8,128)S(1)} %get-tuple-element.108.radial, ...), custom_call_target="tpu_custom_call" | custom-call | tf_op jit(solution)/shard_map/pallas_call | solution.py:730
  60.7 2.5 %collective-permute-done.11.right = f32[96,256]{1,0:T(8,128)S(1)} collective-permute-done((f32[96,256]{1,0:T(8,128)S(1)}, f32[96,256]{1,0:T(8,128)S(1)}, u32[]{:S(2)}, u32[]{:S(2)}) %collective-permute-start.11) | collective-permute-done | bytes 98336 | tf_op jit(solution)/shard_map/ppermute | solution.py:635
  63.2 2.8 %shard_map.131 = (f32[512,256]{1,0:T(8,128)S(1)}, f32[512,128]{1,0:T(8,128)S(1)}, f32[3,128]{1,0:T(4,128)S(1)}, f32[3,128]{1,0:T(4,128)S(1)}, f32[2,128]{1,0:T(2,128)S(1)}) custom-call(s32[65]{0:T(128)S(1)} %get-tuple-element.87.plan.plan_ghost, bf16[512,256]{1,0:T(8,128)(2,1)S(1)} %get-tuple-element.86.hot, f32[512,8]{1,0:T(8,128)S(1)} %get-tuple-element.88.prc, ...), custom_call_target="tpu_custom_call" | custom-call | tf_op jit(solution)/shard_map/pallas_call | solution.py:733
  66.1 2.0 %collective-permute-start.13 = (f32[3,128]{1,0:T(4,128)S(1)}, f32[3,128]{1,0:T(4,128)S(1)}, u32[]{:S(2)}, u32[]{:S(2)}) collective-permute-start(f32[3,128]{1,0:T(4,128)S(1)} %get-tuple-element.132), channel_id=1, source_target_pairs={{0,7},{1,0},{2,1},{3,2},{4,3},{5,4},{6,5},{7,6},{8,15},{9,8},{10,9... | collective-permute-start | bytes 4616 | tf_op jit(solution)/shard_map/ppermute | solution.py:631
  68.1 1.6 %collective-permute-done.12.up = f32[3,128]{1,0:T(4,128)S(1)} collective-permute-done((f32[3,128]{1,0:T(4,128)S(1)}, f32[3,128]{1,0:T(4,128)S(1)}, u32[]{:S(2)}, u32[]{:S(2)}) %collective-permute-start.12) | collective-permute-done | bytes 1568 | tf_op jit(solution)/shard_map/ppermute | solution.py:630
  69.7 2.2 %collective-permute-done.13.down = f32[3,128]{1,0:T(4,128)S(1)} collective-permute-done((f32[3,128]{1,0:T(4,128)S(1)}, f32[3,128]{1,0:T(4,128)S(1)}, u32[]{:S(2)}, u32[]{:S(2)}) %collective-permute-start.13) | collective-permute-done | bytes 1568 | tf_op jit(solution)/shard_map/ppermute | solution.py:631
  71.9 1.8 %collective-permute-start.14 = (f32[3,128]{1,0:T(4,128)S(1)}, f32[3,128]{1,0:T(4,128)S(1)}, u32[]{:S(2)}, u32[]{:S(2)}) collective-permute-start(f32[3,128]{1,0:T(4,128)S(1)} %pad_maximum_fusion.6), channel_id=1, source_target_pairs={{0,248},{8,0},{16,8},{24,16},{32,24},{40,32},{48,40},{56,48},{64,5... | collective-permute-start | bytes 4616 | tf_op jit(solution)/shard_map/ppermute | solution.py:634
  73.8 6.0 %shard_map.132 = (f32[3,512]{1,0:T(4,128)S(1)}, f32[1,512]{1,0:T(1,128)}) custom-call(s32[65]{0:T(128)S(1)} %get-tuple-element.93.plan_own.plan, f32[512,8]{1,0:T(8,128)S(1)} %get-tuple-element.88.prc, f32[16,8,128]{2,1,0:T(8,128)S(1)} %get-tuple-element.94.xt, f32[512,256]{1,0:T(8,128)S(1)} %get-tuple-element.133.quad, ...), custom_call_target="tpu_custom_call" | custom-call | tf_op jit(solution)/shard_map/pallas_call | solution.py:741
  79.7 0.6 collective-permute-done.15.right
  80.4 0.9 %shard_map.133 = f32[3,512]{1,0:T(4,128)} custom-call(bf16[512,256]{1,0:T(8,128)(2,1)S(1)} %get-tuple-element.86.hot, f32[3,128]{1,0:T(4,128)S(1)} %collective-permute-done.14.left, f32[3,128]{1,0:T(4,128)S(1)} %collective-permute-done.15.right, f32[3,128]{1,0:T(4,128)S(1)} %collective-permute-done.12.up, f32[3,128]{1,0:T(4,128)S(1)} %collective-permute-done.13.down, ...), custom_call_target="tpu_custom_call" | custom-call | tf_op jit(solution)/shard_map/pallas_call | solution.py:747
  (31 shorter events, 0.9 us)
Async XLA Ops:
  1.8 5.1 %collective-permute-start = (f32[3,128]{1,0:T(4,128)S(1)}, f32[3,128]{1,0:T(4,128)S(1)}, u32[]{:S(2)}, u32[]{:S(2)}) collective-permute-start(f32[3,128]{1,0:T(4,128)S(1)} %get-tuple-element.70), channel_id=1, source_target_pairs={{0,1},{1,2},{2,3},{3,4},{4,5},{5,6},{6,7},{7,0},{8,9},{9,10},{10,1... | collective-permute-start | bytes 4616 | tf_op jit(solution)/shard_map/ppermute | solution.py:630
  3.0 5.7 %collective-permute-start.1 = (f32[3,128]{1,0:T(4,128)S(1)}, f32[3,128]{1,0:T(4,128)S(1)}, u32[]{:S(2)}, u32[]{:S(2)}) collective-permute-start(f32[3,128]{1,0:T(4,128)S(1)} %get-tuple-element.71), channel_id=1, source_target_pairs={{0,7},{1,0},{2,1},{3,2},{4,3},{5,4},{6,5},{7,6},{8,15},{9,8},{10,9... | collective-permute-start | bytes 4616 | tf_op jit(solution)/shard_map/ppermute | solution.py:631
  8.7 8.9 %collective-permute-start.2 = (f32[3,128]{1,0:T(4,128)S(1)}, f32[3,128]{1,0:T(4,128)S(1)}, u32[]{:S(2)}, u32[]{:S(2)}) collective-permute-start(f32[3,128]{1,0:T(4,128)S(1)} %pad_maximum_fusion.4), channel_id=1, source_target_pairs={{0,248},{8,0},{16,8},{24,16},{32,24},{40,32},{48,40},{56,48},{64,5... | collective-permute-start | bytes 4616 | tf_op jit(solution)/shard_map/ppermute | solution.py:634
  14.8 6.7 %collective-permute-start.3 = (f32[3,128]{1,0:T(4,128)S(1)}, f32[3,128]{1,0:T(4,128)S(1)}, u32[]{:S(2)}, u32[]{:S(2)}) collective-permute-start(f32[3,128]{1,0:T(4,128)S(1)} %pad_maximum_fusion.5), channel_id=1, source_target_pairs={{0,8},{8,16},{16,24},{24,32},{32,40},{40,48},{48,56},{56,64},{64,7... | collective-permute-start | bytes 4616 | tf_op jit(solution)/shard_map/ppermute | solution.py:635
  24.8 4.7 %collective-permute-start.4 = (f32[96,256]{1,0:T(8,128)S(1)}, f32[96,256]{1,0:T(8,128)S(1)}, u32[]{:S(2)}, u32[]{:S(2)}) collective-permute-start(f32[96,256]{1,0:T(8,128)S(1)} %get-tuple-element.96), channel_id=1, source_target_pairs={{0,1},{1,2},{2,3},{3,4},{4,5},{5,6},{6,7},{7,0},{8,9},{9,10},{10,1... | collective-permute-start | bytes 294920 | tf_op jit(solution)/shard_map/ppermute | solution.py:630
  26.6 6.7 %collective-permute-start.5 = (f32[96,256]{1,0:T(8,128)S(1)}, f32[96,256]{1,0:T(8,128)S(1)}, u32[]{:S(2)}, u32[]{:S(2)}) collective-permute-start(f32[96,256]{1,0:T(8,128)S(1)} %get-tuple-element.97), channel_id=1, source_target_pairs={{0,7},{1,0},{2,1},{3,2},{4,3},{5,4},{6,5},{7,6},{8,15},{9,8},{10,9... | collective-permute-start | bytes 294920 | tf_op jit(solution)/shard_map/ppermute | solution.py:631
  33.3 4.6 %collective-permute-start.6 = (f32[96,256]{1,0:T(8,128)S(1)}, f32[96,256]{1,0:T(8,128)S(1)}, u32[]{:S(2)}, u32[]{:S(2)}) collective-permute-start(f32[96,256]{1,0:T(8,128)S(1)} %pad_maximum_fusion), channel_id=1, source_target_pairs={{0,248},{8,0},{16,8},{24,16},{32,24},{40,32},{48,40},{56,48},{64,5... | collective-permute-start | bytes 294920 | tf_op jit(solution)/shard_map/ppermute | solution.py:634
  33.5 7.7 %collective-permute-start.7 = (f32[96,256]{1,0:T(8,128)S(1)}, f32[96,256]{1,0:T(8,128)S(1)}, u32[]{:S(2)}, u32[]{:S(2)}) collective-permute-start(f32[96,256]{1,0:T(8,128)S(1)} %pad_maximum_fusion.1), channel_id=1, source_target_pairs={{0,8},{8,16},{16,24},{24,32},{32,40},{40,48},{48,56},{56,64},{64,7... | collective-permute-start | bytes 294920 | tf_op jit(solution)/shard_map/ppermute | solution.py:635
  47.7 4.9 %collective-permute-start.8 = (f32[96,256]{1,0:T(8,128)S(1)}, f32[96,256]{1,0:T(8,128)S(1)}, u32[]{:S(2)}, u32[]{:S(2)}) collective-permute-start(f32[96,256]{1,0:T(8,128)S(1)} %get-tuple-element.120), channel_id=1, source_target_pairs={{0,1},{1,2},{2,3},{3,4},{4,5},{5,6},{6,7},{7,0},{8,9},{9,10},{10,1... | collective-permute-start | bytes 294920 | tf_op jit(solution)/shard_map/ppermute | solution.py:630
  48.0 6.8 %collective-permute-start.9 = (f32[96,256]{1,0:T(8,128)S(1)}, f32[96,256]{1,0:T(8,128)S(1)}, u32[]{:S(2)}, u32[]{:S(2)}) collective-permute-start(f32[96,256]{1,0:T(8,128)S(1)} %get-tuple-element.121), channel_id=1, source_target_pairs={{0,7},{1,0},{2,1},{3,2},{4,3},{5,4},{6,5},{7,6},{8,15},{9,8},{10,9... | collective-permute-start | bytes 294920 | tf_op jit(solution)/shard_map/ppermute | solution.py:631
  54.8 5.8 %collective-permute-start.10 = (f32[96,256]{1,0:T(8,128)S(1)}, f32[96,256]{1,0:T(8,128)S(1)}, u32[]{:S(2)}, u32[]{:S(2)}) collective-permute-start(f32[96,256]{1,0:T(8,128)S(1)} %pad_maximum_fusion.2), channel_id=1, source_target_pairs={{0,248},{8,0},{16,8},{24,16},{32,24},{40,32},{48,40},{56,48},{64,5... | collective-permute-start | bytes 294920 | tf_op jit(solution)/shard_map/ppermute | solution.py:634
  55.5 7.7 %collective-permute-start.11 = (f32[96,256]{1,0:T(8,128)S(1)}, f32[96,256]{1,0:T(8,128)S(1)}, u32[]{:S(2)}, u32[]{:S(2)}) collective-permute-start(f32[96,256]{1,0:T(8,128)S(1)} %pad_maximum_fusion.3), channel_id=1, source_target_pairs={{0,8},{8,16},{16,24},{24,32},{32,40},{40,48},{48,56},{56,64},{64,7... | collective-permute-start | bytes 294920 | tf_op jit(solution)/shard_map/ppermute | solution.py:635
  66.0 3.7 %collective-permute-start.12 = (f32[3,128]{1,0:T(4,128)S(1)}, f32[3,128]{1,0:T(4,128)S(1)}, u32[]{:S(2)}, u32[]{:S(2)}) collective-permute-start(f32[3,128]{1,0:T(4,128)S(1)} %get-tuple-element.130), channel_id=1, source_target_pairs={{0,1},{1,2},{2,3},{3,4},{4,5},{5,6},{6,7},{7,0},{8,9},{9,10},{10,1... | collective-permute-start | bytes 4616 | tf_op jit(solution)/shard_map/ppermute | solution.py:630
  66.1 5.8 %collective-permute-start.13 = (f32[3,128]{1,0:T(4,128)S(1)}, f32[3,128]{1,0:T(4,128)S(1)}, u32[]{:S(2)}, u32[]{:S(2)}) collective-permute-start(f32[3,128]{1,0:T(4,128)S(1)} %get-tuple-element.132), channel_id=1, source_target_pairs={{0,7},{1,0},{2,1},{3,2},{4,3},{5,4},{6,5},{7,6},{8,15},{9,8},{10,9... | collective-permute-start | bytes 4616 | tf_op jit(solution)/shard_map/ppermute | solution.py:631
  71.9 7.8 %collective-permute-start.14 = (f32[3,128]{1,0:T(4,128)S(1)}, f32[3,128]{1,0:T(4,128)S(1)}, u32[]{:S(2)}, u32[]{:S(2)}) collective-permute-start(f32[3,128]{1,0:T(4,128)S(1)} %pad_maximum_fusion.6), channel_id=1, source_target_pairs={{0,248},{8,0},{16,8},{24,16},{32,24},{40,32},{48,40},{56,48},{64,5... | collective-permute-start | bytes 4616 | tf_op jit(solution)/shard_map/ppermute | solution.py:634
  73.7 6.7 %collective-permute-start.15 = (f32[3,128]{1,0:T(4,128)S(1)}, f32[3,128]{1,0:T(4,128)S(1)}, u32[]{:S(2)}, u32[]{:S(2)}) collective-permute-start(f32[3,128]{1,0:T(4,128)S(1)} %pad_maximum_fusion.7), channel_id=1, source_target_pairs={{0,8},{8,16},{16,24},{24,32},{32,40},{40,48},{48,56},{56,64},{64,7... | collective-permute-start | bytes 4616 | tf_op jit(solution)/shard_map/ppermute | solution.py:635
